TPU v7x, 256 devices: a whole 4x4x8 slice. The times are simulated.
256 devices in a mesh: ep: 64 (over z, x, core), tp: 4 (over y).
Axes of the slice: x: 4, y: 4, z: 8, core: 2. Of those that a mesh axis runs over, the one named last changes fastest.
Arguments:
- tokens: bfloat16 [8192, 2048], P('ep', 'tp'), may hold values from -6 to 6
- cotangent: bfloat16 [8192, 2048], P('ep', 'tp'), may hold values from -12 to 12
- route_weights: bfloat16 [8192, 8], P('ep'), may hold values from 0.049804688 to 0.59765625
- routes: int32 [8192, 8], P('ep'), may hold values from 0 to 63, all different within a row; in each aligned block of 128 rows (0 to 127, 128 to 255, ...) at most 24 rows name the same one
- grid_gate: bfloat16 [64, 768, 2048], P('ep', 'tp'), may hold values from -4 to 4
- latent_gate: bfloat16 [64, 768, 2048], P('ep', 'tp'), may hold values from -0.5 to 0.5
- scale_gate: float32 [64, 768], P('ep', 'tp'), may hold values from 0.006 to 0.02
- grid_up: bfloat16 [64, 768, 2048], P('ep', 'tp'), may hold values from -4 to 4
- latent_up: bfloat16 [64, 768, 2048], P('ep', 'tp'), may hold values from -0.5 to 0.5
- scale_up: float32 [64, 768], P('ep', 'tp'), may hold values from 0.006 to 0.02
- grid_down: bfloat16 [64, 768, 2048], P('ep', 'tp'), may hold values from -4 to 4
- latent_down: bfloat16 [64, 768, 2048], P('ep', 'tp'), may hold values from -0.5 to 0.5
- scale_down: float32 [64, 2048], P('ep'), may hold values from 0.006 to 0.02
Outputs:
- grad_latent_gate: float32 [64, 768, 2048], P('ep', 'tp')
- grad_latent_up: float32 [64, 768, 2048], P('ep', 'tp')
- grad_latent_down: float32 [64, 768, 2048], P('ep', 'tp')
- token_grad: bfloat16 [8192, 2048], P('ep', 'tp')
- route_grad: float32 [8192, 8], P('ep')
Inputs may be any that keep to these rules, and one draw needn't show every extreme that they name: `routes`: each row names 8 different experts. In each aligned block of 128 tokens (the tokens of one index of ep), no expert is named by more than 24 of them, a bound that some block reaches.
All inputs are finite; a program needn't handle non-finite values.
Results may differ from a plain program's by a relative error of at most 0.006.
Values may be sent and summed in bfloat16 or wider, within the bound.
A program may use at most 192 MiB of HBM per device.

v0:
```python
import jax
import jax.numpy as jnp
from jax import lax
from jax.sharding import PartitionSpec as P

temper = 0.25
grad_factor = 8.0


def sent_together(arrays, axis, split_dim, concat_dim, along):
    columns = [a.reshape(*a.shape[:along], -1) for a in arrays]
    both = jnp.concatenate(columns, axis=along)
    whole, at, gathered = (
        lax.all_to_all(both, axis, split_axis=split_dim, concat_axis=concat_dim, tiled=True),
        0,
        [],
    )
    for a, column in zip(arrays, columns):
        section = whole[..., at : at + column.shape[along]]
        gathered.append(section.reshape(*section.shape[:along], *a.shape[along:]))
        at += column.shape[along]
    return tuple(gathered)


def side_by_side(arrays, axis, dim, along):
    ends, at = ([], 0)
    for a in arrays[:-1]:
        at += a.shape[along]
        ends.append(at)
    both = jnp.concatenate(arrays, axis=along)
    return tuple(jnp.split(lax.all_gather(both, axis, axis=dim, tiled=True), ends, axis=along))


def copy_for_each(value, axis):
    peers = lax.axis_size(axis)
    return lax.all_to_all(
        jnp.broadcast_to(value[None], (peers, *value.shape)), axis, 0, 0, tiled=True
    )


def taken_together(value, axis):
    everything = copy_for_each(value, axis)
    return jnp.sum(everything, axis=0)


def soften_rows(grid, latent, scale):
    level = grid.astype(jnp.float32) + 0.5 * (1.0 + jnp.tanh(latent.astype(jnp.float32) / temper))
    return level * scale[:, None]


def soften_cols(grid, latent, scale):
    level = grid.astype(jnp.float32) + 0.5 * (1.0 + jnp.tanh(latent.astype(jnp.float32) / temper))
    return level * scale[None, :]


def latent_rows(grad_weight, latent, scale):
    slope = jnp.tanh(latent.astype(jnp.float32) / temper)
    return grad_factor * grad_weight * scale[:, None] * (1.0 - slope * slope) / (2.0 * temper)


def latent_cols(grad_weight, latent, scale):
    slope = jnp.tanh(latent.astype(jnp.float32) / temper)
    return grad_factor * grad_weight * scale[None, :] * (1.0 - slope * slope) / (2.0 * temper)


def block_slots(block_routes, experts, capacity):
    flat = block_routes.reshape(-1)
    columns = jnp.arange(experts, dtype=jnp.int32)
    onehot = (flat[:, None] == columns[None, :]).astype(jnp.int32)
    earlier = jnp.cumsum(onehot, axis=0) - onehot
    return flat * capacity + jnp.sum(earlier * onehot, axis=1)


def expert_backward(rows_x, rows_y, rows_p, w_gate, w_up, w_down):
    rowwise = (((1,), (1,)), ((), ()))
    gate = lax.dot_general(rows_x, w_gate, rowwise, preferred_element_type=jnp.float32)
    upper = lax.dot_general(rows_x, w_up, rowwise, preferred_element_type=jnp.float32)
    sigma = jax.nn.sigmoid(gate)
    active = gate * sigma
    hidden = active * upper
    weight = rows_p.astype(jnp.float32)[:, None]
    scaled = (hidden * weight).astype(jnp.bfloat16)
    back_hidden = lax.dot_general(rows_y, w_down, rowwise, preferred_element_type=jnp.float32)
    score = jnp.sum(hidden * back_hidden, axis=1)
    delta = back_hidden * weight
    grad_gate = (delta * upper * sigma * (1.0 + gate * (1.0 - sigma))).astype(jnp.bfloat16)
    grad_upper = (delta * active).astype(jnp.bfloat16)
    contract = (((0,), (0,)), ((), ()))
    grad_wg = lax.dot_general(grad_gate, rows_x, contract, preferred_element_type=jnp.float32)
    grad_wu = lax.dot_general(grad_upper, rows_x, contract, preferred_element_type=jnp.float32)
    grad_wd = lax.dot_general(scaled, rows_y, contract, preferred_element_type=jnp.float32)
    back_rows = jnp.dot(grad_gate, w_gate, preferred_element_type=jnp.float32)
    back_rows = back_rows + jnp.dot(grad_upper, w_up, preferred_element_type=jnp.float32)
    return (grad_wg, grad_wu, grad_wd, back_rows, score)


def pad_rows(values):
    return jnp.concatenate([values, jnp.zeros((1, values.shape[1]), values.dtype)], axis=0)


def body(
    tokens,
    cotangent,
    route_weights,
    routes,
    grid_gate,
    latent_gate,
    scale_gate,
    grid_up,
    latent_up,
    scale_up,
    grid_down,
    latent_down,
    scale_down,
):
    n_ep = lax.axis_size("ep")
    experts = n_ep * grid_gate.shape[0]
    tok_rows, top = routes.shape
    capacity = min(tok_rows, 3 * tok_rows * top // (2 * experts))
    entries = tok_rows * top
    dest = block_slots(routes, experts, capacity)
    table = (
        jnp.full((experts * capacity,), entries, jnp.int32)
        .at[dest]
        .set(jnp.arange(entries, dtype=jnp.int32))
    )
    token_table = table // top
    weights_pad = jnp.concatenate(
        [route_weights.reshape(-1), jnp.zeros((1,), jnp.bfloat16)], axis=0
    )
    send_weights = weights_pad[table].reshape(experts, capacity)
    w_gate = soften_rows(grid_gate[0], latent_gate[0], scale_gate[0]).astype(jnp.bfloat16)
    w_up = soften_rows(grid_up[0], latent_up[0], scale_up[0]).astype(jnp.bfloat16)
    w_down = soften_cols(grid_down[0], latent_down[0], scale_down[0]).astype(jnp.bfloat16)
    part_x = pad_rows(tokens)[token_table].reshape(experts, capacity, -1)
    part_y = pad_rows(cotangent)[token_table].reshape(experts, capacity, -1)
    some_x, some_y, got_p = sent_together((part_x, part_y, send_weights), "ep", 0, 0, 2)
    got_x, got_y = side_by_side((some_x, some_y), "tp", 2, 0)
    width = got_x.shape[2]
    rows_x = got_x.reshape(-1, width)
    rows_y = got_y.reshape(-1, width)
    rows_p = got_p.reshape(-1)
    grad_wg, grad_wu, grad_wd, back_rows, score = expert_backward(
        rows_x, rows_y, rows_p, w_gate, w_up, w_down
    )
    grad_gate = latent_rows(grad_wg, latent_gate[0], scale_gate[0])[None]
    grad_upper = latent_rows(grad_wu, latent_up[0], scale_up[0])[None]
    grad_lower = latent_cols(grad_wd, latent_down[0], scale_down[0])[None]
    score = taken_together(score.reshape(n_ep, capacity), "tp")
    back_rows = back_rows.reshape(n_ep, capacity, width)
    share = lax.psum_scatter(back_rows, "tp", scatter_dimension=2, tiled=True)
    came_rows, came_score = (
        lax.all_to_all(share, "ep", split_axis=0, concat_axis=0, tiled=True),
        lax.all_to_all(score, "ep", split_axis=0, concat_axis=0, tiled=True),
    )
    flat_rows = came_rows.reshape(experts * capacity, share.shape[2])
    token_grad = jnp.sum(flat_rows[dest].reshape(tok_rows, top, share.shape[2]), axis=1).astype(
        jnp.bfloat16
    )
    route_grad = came_score.reshape(-1)[dest].reshape(tok_rows, top)
    return (grad_gate, grad_upper, grad_lower, token_grad, route_grad)


def solution(mesh):
    return jax.shard_map(
        body,
        mesh=mesh,
        in_specs=(
            P("ep", "tp"),
            P("ep", "tp"),
            P("ep", None),
            P("ep", None),
            P("ep", "tp", None),
            P("ep", "tp", None),
            P("ep", "tp"),
            P("ep", "tp", None),
            P("ep", "tp", None),
            P("ep", "tp"),
            P("ep", "tp", None),
            P("ep", "tp", None),
            P("ep", None),
        ),
        out_specs=(
            P("ep", "tp", None),
            P("ep", "tp", None),
            P("ep", "tp", None),
            P("ep", "tp"),
            P("ep", None),
        ),
        check_vma=False,
    )
```

profile of v0, /device:TPU:38, one launch (start us, length us, event | category | flops | bytes accessed | tf_op | source)
XLA Modules:
  0.0 508.9 jit_solution(12305425227418247731)
XLA Ops:
  8.9 0.8 copy.49
  10.0 0.9 concatenate.15
  10.9 0.9 concatenate.16
  11.8 18.0 %reduce-window.6 = s32[64,8,128]{2,1,0:T(8,128)S(1)} reduce-window(s32[64,8,128]{2,1,0:T(8,128)S(1)} %fusion.49, s32[]{:T(128)} %constant.40.clone.1), window={size=1x1x128 pad=0_0x0_0x127_0}, to_apply=%region_0.0 | reduce-window | flops 8323072 | bytes 524292 | tf_op jit(solution)/shard_map/reduce-window
  30.5 4.3 scatter_custom_fusion
  34.9 9.5 %gather_fusion.2 = bf16[1536]{0:T(1024)(128)(2,1)S(1)} fusion(bf16[1025]{0:T(1024)(128)(2,1)S(1)} %pad_maximum_fusion.2, s32[2048]{0:T(1024)S(1)} %get-tuple-element.34), kind=kCustom, calls=%fused_computation.2 | custom fusion | bytes 12288 | tf_op jit(solution)/shard_map/gather | solution.py:131
  44.4 1.5 reshape_reshape.5
  45.8 4.8 gather_fusion.1
  50.6 4.8 gather_fusion
  55.4 1.3 pad_maximum_fusion
  56.7 92.6 %all_to_all.24 = bf16[64,24,1025]{2,1,0:T(8,128)(2,1)S(1)} all-to-all(bf16[64,24,1025]{2,1,0:T(8,128)(2,1)S(1)} %pad_maximum_fusion), channel_id=1, replica_groups=mesh['ep'=64,'tp'=4] {'ep'}, dimensions={0} | all-to-all | bytes 6297600 | tf_op jit(solution)/shard_map/all_to_all | solution.py:14
  149.6 1.9 pad_maximum_fusion.1
  151.8 0.9 convert_reduce_fusion
  152.7 0.8 reshape.154
  153.6 116.6 %all-gather.2.cloned.1.call-done = bf16[128,24,2048]{2,1,0:T(8,128)(2,1)} async-done(((bf16[128,24,512]{2,1,0:T(8,128)(2,1)}), bf16[128,24,2048]{2,1,0:T(8,128)(2,1)}) %all-gather.2.cloned.1.call-update) | async-done | bytes 12582928 | tf_op jit(solution)/shard_map/all_gather | solution.py:31
  270.1 5.6 %fusion.70 = (bf16[64,24,2048]{2,1,0:T(8,128)(2,1)S(1)}, bf16[64,24,2048]{2,1,0:T(8,128)(2,1)S(1)}) fusion(bf16[128,24,2048]{2,1,0:T(8,128)(2,1)} %all-gather.2.cloned.1.call-done), kind=kLoop, calls=%fused_computation.113 | loop fusion | bytes 25165824 | tf_op jit(solution)/shard_map/split | solution.py:31
  275.9 2.3 fusion.19
  278.5 2.3 fusion.16
  281.3 2.8 multiply_reduce_fusion
  284.2 1.9 fusion.21
  286.2 6.6 %convolution_add_fusion = f32[1536,2048]{1,0:T(8,128)} fusion(f32[1536,2048]{1,0:T(8,128)S(1)} %fusion.21, bf16[1536,192]{0,1:T(8,128)(2,1)S(1)} %get-tuple-element.31, bf16[1,192,2048]{2,1,0:T(8,128)(2,1)S(1)} %copy-done.7, bf16[1,192,2048]{2,1,0:T(8,128)(2,1)S(1)} %copy-done.5, f32[192]{0:T(256)S(1)} %bitcast.99), kind=kOutput, calls=%fused_computation.6 | convolution fusion | flops 1214251008 | bytes 27329280 | tf_op jit(solution)/shard_map/dot_general | solution.py:93
  293.0 9.2 %all_to_all.25 = f32[4,1,1536]{2,1,0:T(1,128)S(1)} all-to-all(f32[4,1,1536]{2,1,0:T(1,128)S(1)} %reshape.232), channel_id=1, replica_groups=mesh['ep'=64,'tp'=4] {'tp'}, dimensions={0} | all-to-all | bytes 49152 | tf_op jit(solution)/shard_map/all_to_all | solution.py:36
  303.7 17.4 %all_to_all.26 = f32[64,1,24]{2,1,0:T(1,128)S(1)} all-to-all(f32[64,1,24]{2,1,0:T(1,128)S(1)} %copy.52), channel_id=1, replica_groups=mesh['ep'=64,'tp'=4] {'ep'}, dimensions={0} | all-to-all | bytes 12288 | tf_op jit(solution)/shard_map/all_to_all | solution.py:154
  321.1 90.0 %reduce-scatter.2.cloned.1.call-done = f32[64,24,512]{2,1,0:T(8,128)} async-done(((f32[64,24,2048]{2,1,0:T(8,128)}), f32[64,24,512]{2,1,0:T(8,128)}) %reduce-scatter.2.cloned.1.call-update) | async-done | bytes 3145744 | tf_op jit(solution)/shard_map/reduce_scatter | solution.py:151
  411.1 10.4 %all-to-all-start.1 = ((f32[64,24,512]{2,1,0:T(8,128)}), f32[64,24,512]{2,1,0:T(8,128)S(1)}, u32[]{:S(2)}, u32[]{:S(2)}) async-start(f32[64,24,512]{2,1,0:T(8,128)} %reduce-scatter.2.cloned.1.call-done), calls=%async_computation.2 | async-start | bytes 6291456 | tf_op jit(solution)/shard_map/all_to_all | solution.py:153
  421.6 5.9 %fusion.2 = f32[1,192,2048]{2,1,0:T(8,128)} fusion(bf16[1536,192]{0,1:T(8,128)(2,1)} %copy-done.9, bf16[1536,2048]{1,0:T(8,128)(2,1)} %bitcast.88, bf16[1,192,2048]{2,1,0:T(8,128)(2,1)} %param.18, f32[192]{0:T(256)S(1)} %broadcast_multiply_fusion.3), kind=kOutput, calls=%fused_computation.14 | convolution fusion | flops 1210712064 | bytes 9241344 | tf_op jit(solution)/shard_map/dot_general | solution.py:89
  427.5 5.6 %fusion.5 = f32[1,192,2048]{2,1,0:T(8,128)} fusion(bf16[1536,192]{0,1:T(8,128)(2,1)S(1)} %copy-done.3, bf16[1536,2048]{1,0:T(8,128)(2,1)} %bitcast.89, bf16[1,192,2048]{2,1,0:T(8,128)(2,1)S(1)} %copy-done.8, f32[192]{0:T(256)S(1)} %broadcast_multiply_fusion.2), kind=kOutput, calls=%fused_computation.17 | convolution fusion | flops 1210712064 | bytes 9241344 | tf_op jit(solution)/shard_map/dot_general | solution.py:90
  433.1 5.7 %fusion.8 = f32[1,192,2048]{2,1,0:T(8,128)} fusion(bf16[1536,2048]{1,0:T(8,128)(2,1)} %bitcast.85, bf16[1,192,2048]{2,1,0:T(8,128)(2,1)S(1)} %copy-done.15, f32[2048]{0:T(1024)S(1)} %broadcast_multiply_fusion, f32[1536]{0:T(1024)S(1)} %reshape.154, f32[1536,192]{0,1:T(8,128)S(1)} %copy-done.19, f32[1536,192]{0,1:T(8,128)S(1)} %copy-done.17), kind=kOutput, calls=%fused_computation.20 | convolution fusion | flops 1212776448 | bytes 11024384 | tf_op jit(solution)/shard_map/dot_general | solution.py:91
  440.1 6.2 %gather_fusion.4 = f32[1024]{0:T(1024)S(1)} fusion(f32[1536]{0:T(1024)S(1)} %reshape.152, s32[1024]{0:T(1024)S(1)} %broadcast_clamp_fusion), kind=kCustom, calls=%fused_computation.4 | custom fusion | bytes 12288 | tf_op jit(solution)/shard_map/gather | solution.py:160
  447.0 47.4 %all-to-all-done.1 = f32[64,24,512]{2,1,0:T(8,128)S(1)} async-done(((f32[64,24,512]{2,1,0:T(8,128)}), f32[64,24,512]{2,1,0:T(8,128)S(1)}, u32[]{:S(2)}, u32[]{:S(2)}) %all-to-all-start.1) | async-done | bytes 3145760 | tf_op jit(solution)/shard_map/all_to_all | solution.py:153
  494.4 4.9 gather_fusion.3
  499.3 2.8 bitcast_reduce_fusion
  (83 shorter events, 7.8 us)
Async XLA Ops:
  7.2 263.0 %all-gather.2.cloned.1.call-start = ((), (), s32[]{:S(2)}) async-start(), calls=%async_computation.5 | async-start | bytes 15728640 | tf_op jit(solution)/shard_map/all_gather | solution.py:31
  151.6 259.5 %reduce-scatter.2.cloned.1.call-start = ((), (), s32[]{:S(2)}) async-start(), calls=%async_computation.6 | async-start | bytes 15728640 | tf_op jit(solution)/shard_map/reduce_scatter | solution.py:151
  153.5 122.3 %copy-start.4 = (bf16[1,192,2048]{2,1,0:T(8,128)(2,1)S(1)}, bf16[1,192,2048]{2,1,0:T(8,128)(2,1)}, u32[]{:S(2)}) copy-start(bf16[1,192,2048]{2,1,0:T(8,128)(2,1)} %param.17) | copy-start | bytes 2359300
  153.6 122.3 %copy-start.6 = (bf16[1,192,2048]{2,1,0:T(8,128)(2,1)S(1)}, bf16[1,192,2048]{2,1,0:T(8,128)(2,1)}, u32[]{:S(2)}) copy-start(bf16[1,192,2048]{2,1,0:T(8,128)(2,1)} %param.18) | copy-start | bytes 2359300
  153.6 122.3 %copy-start.12 = (f32[1,192]{1,0:T(1,128)S(1)}, f32[1,192]{1,0:T(1,128)}, u32[]{:S(2)}) copy-start(f32[1,192]{1,0:T(1,128)} %param.19) | copy-start | bytes 2308
  275.8 2.7 copy-start.1
  275.8 5.2 %copy-start = (bf16[64,24,2048]{2,1,0:T(8,128)(2,1)}, bf16[64,24,2048]{2,1,0:T(8,128)(2,1)S(1)}, u32[]{:S(2)}) copy-start(bf16[64,24,2048]{2,1,0:T(8,128)(2,1)S(1)} %get-tuple-element.25) | copy-start | bytes 18874372
  275.8 2.6 copy-start.5
  275.8 2.6 copy-start.7
  275.9 2.6 copy-start.11
  278.2 3.1 copy-start.16
  278.5 2.8 copy-start.10
  278.5 2.8 copy-start.13
  278.5 2.8 copy-start.14
  280.8 3.4 copy-start.18
  284.2 2.0 copy-start.9
  284.2 2.0 copy-start.2
  411.1 83.3 %all-to-all-start.1 = ((f32[64,24,512]{2,1,0:T(8,128)}), f32[64,24,512]{2,1,0:T(8,128)S(1)}, u32[]{:S(2)}, u32[]{:S(2)}) async-start(f32[64,24,512]{2,1,0:T(8,128)} %reduce-scatter.2.cloned.1.call-done), calls=%async_computation.2 | async-start | bytes 6291456 | tf_op jit(solution)/shard_map/all_to_all | solution.py:153
  421.5 5.9 %copy-start.3 = (bf16[1536,192]{0,1:T(8,128)(2,1)S(1)}, bf16[1536,192]{0,1:T(8,128)(2,1)}, u32[]{:S(2)}) copy-start(bf16[1536,192]{0,1:T(8,128)(2,1)} %copy-done.2) | copy-start | bytes 1769476
  421.5 5.9 %copy-start.8 = (bf16[1,192,2048]{2,1,0:T(8,128)(2,1)S(1)}, bf16[1,192,2048]{2,1,0:T(8,128)(2,1)}, u32[]{:S(2)}) copy-start(bf16[1,192,2048]{2,1,0:T(8,128)(2,1)} %param.21) | copy-start | bytes 2359300
  427.4 5.7 %copy-start.15 = (bf16[1,192,2048]{2,1,0:T(8,128)(2,1)S(1)}, bf16[1,192,2048]{2,1,0:T(8,128)(2,1)}, u32[]{:S(2)}) copy-start(bf16[1,192,2048]{2,1,0:T(8,128)(2,1)} %param.24) | copy-start | bytes 2359300
  427.4 5.7 %copy-start.17 = (f32[1536,192]{0,1:T(8,128)S(1)}, f32[1536,192]{0,1:T(8,128)}, u32[]{:S(2)}) copy-start(f32[1536,192]{0,1:T(8,128)} %copy-done.16) | copy-start | bytes 3538948
  427.4 5.7 %copy-start.19 = (f32[1536,192]{0,1:T(8,128)S(1)}, f32[1536,192]{0,1:T(8,128)}, u32[]{:S(2)}) copy-start(f32[1536,192]{0,1:T(8,128)} %copy-done.18) | copy-start | bytes 3538948
Sparse Core Ops, SparseCore 0:
  151.7 118.3 all-gather.1
  292.9 118.1 reduce-scatter.1
where the time goes:
time: 511 us; the launch traced here: 509 us
  waiting for transfers between devices  254 us (50%)
  blocking collectives  119 us (23%)
  local copies, waits for them, and re-layouts  50 us (10%)
  matrix products  33.1 us (6%)
  other arithmetic  27.3 us (5%)
  between operations  14.5 us (3%)
  starting transfers between devices  10.7 us (2%)
    all_gather x1, waiting for transfers between devices, side_by_side(): lax.all_gather(both, axis, axis=dim, tiled=True)  117 us
    all_to_all x1, blocking collectives, sent_together(): lax.all_to_all(both, axis, split_axis=split_dim, concat_axis=concat_dim,...  92.6 us
    reduce_scatter x1, waiting for transfers between devices, body(): share = lax.psum_scatter(back_rows, 'tp', scatter_dimension=2, tiled=True)  90 us
    all_to_all x1, waiting for transfers between devices, body(): lax.all_to_all(share, 'ep', split_axis=0, concat_axis=0, tiled=True)  47.4 us
    another operation x3, other arithmetic  18.2 us
    all_to_all x1, blocking collectives, body(): lax.all_to_all(score, 'ep', split_axis=0, concat_axis=0, tiled=True)  17.4 us
    all_to_all x1, starting transfers between devices, body(): lax.all_to_all(share, 'ep', split_axis=0, concat_axis=0, tiled=True)  10.4 us
  transfers between devices with their start and end apart: 3, of which 3 were waited for; matrix products, arithmetic and copies ran while one was open for 6% of the time, Pallas kernels for 0%

commit v1 on v0

v1 whole, which is shorter than its diff:
```python
import jax
import jax.numpy as jnp
from jax import lax
from jax.experimental import pallas as pl
from jax.experimental.pallas import tpu as pltpu
from jax.sharding import PartitionSpec as P

temper = 0.25
grad_factor = 8.0

NZ, NX, NY = 8, 4, 4
D, FF, TOK, EXPERTS, CAP = 2048, 768, 128, 64, 24
QD = D // NY
HID = FF // NY
HALF = HID // 2
PAIR = 2 * CAP
ROWS = NX * 2 * PAIR
WIDE = 2 * D + 128
BACK = D + 128
F32, BF16 = jnp.float32, jnp.bfloat16
MESH = pl.DeviceIdType.MESH


def dot_nt(a, b):
    return lax.dot_general(a, b, (((1,), (1,)), ((), ())), preferred_element_type=F32)


def dot_tn(a, b):
    return lax.dot_general(a, b, (((0,), (0,)), ((), ())), preferred_element_type=F32)


def dot_nn(a, b):
    return lax.dot_general(a, b, (((1,), (0,)), ((), ())), preferred_element_type=F32)


def kernel(
    tok_ref, cot_ref, rt_ref, wt_ref, routes_ref, wg_ref, wu_ref, wd_ref,
    sums_ref, tgrad_ref, rgrad_ref,
    wf, grad, rr, blk, aux, sendbuf, rows, smat, gs, us, ap, dg, du, br, rb, part, zb, zt, fb, stage, tg, sc, fin,
    ws, wr, wl, gsend, grecv, ys, yr, zs, zr, xs, xr, bs, brecv, zbs, zbr, ls, lr,
):
    i, y = lax.axis_index("ep"), lax.axis_index("tp")
    z, x, c = i // 8, lax.rem(i, 8) // 2, lax.rem(i, 2)
    own = 2 * x + c
    column = c == y // 2
    odd = lax.rem(z + y, 2) == 1
    yb = 2 * c + lax.rem(z, 2)
    owner = y == yb

    def up(n):
        return lax.rem(y + n + NY, NY)

    def zat(n):
        return lax.rem(z + n + NZ, NZ)

    def zdev(n):
        return (8 * zat(n) + own, y)

    def remote(src, dst, send, recv, dev):
        return pltpu.make_async_remote_copy(
            src_ref=src, dst_ref=dst, send_sem=send, recv_sem=recv, device_id=dev, device_id_type=MESH
        )

    def arrived(dst, recv, send):
        remote(dst, dst, send, recv, (i, up(1))).wait_recv()

    def sent(src, send, recv):
        remote(src, src, send, recv, (i, up(1))).wait_send()

    def mult(v, n):
        return pl.multiple_of(v, n)

    barrier = pltpu.get_barrier_semaphore()
    for d in range(1, NY):
        pl.semaphore_signal(barrier, inc=1, device_id=(i, up(d)), device_id_type=MESH)
    for d in (1, -1):
        pl.semaphore_signal(barrier, inc=1, device_id=zdev(d), device_id_type=MESH)
    for d in range(1, 8):
        pl.semaphore_signal(barrier, inc=1, device_id=(8 * z + lax.rem(own + d, 8), y), device_id_type=MESH)

    weights = (wg_ref, wu_ref, wd_ref)
    stage[:, 0:QD] = tok_ref[...]
    stage[:, QD:] = cot_ref[...]

    def block(s, f):
        return blk.at[s // 2, f, pl.ds(mult(TOK * lax.rem(s, 2), TOK), TOK), :]

    s_own = z // 2

    @pl.when(owner)
    def _():
        expert = lax.broadcasted_iota(jnp.int32, (EXPERTS, TOK), 0)
        hit = jnp.zeros((EXPERTS, TOK), F32)
        weight = jnp.zeros((EXPERTS, TOK), F32)
        for k in range(8):
            same = expert == rt_ref[k : k + 1, :]
            hit = hit + jnp.where(same, 1.0, 0.0)
            weight = weight + jnp.where(same, wt_ref[k : k + 1, :], 0.0)
        before = lax.broadcasted_iota(jnp.int32, (TOK, TOK), 0) < lax.broadcasted_iota(jnp.int32, (TOK, TOK), 1)
        slot = dot_nn(hit.astype(BF16), jnp.where(before, 1.0, 0.0).astype(BF16))
        aux[s_own, 0:EXPERTS, :] = jnp.where(hit > 0.0, slot, -100.0)
        aux[s_own, EXPERTS:, :] = weight

    pl.semaphore_wait(barrier, 3 + 2 + 7)

    @pl.when(jnp.logical_not(owner))
    def _():
        remote(stage, block(s_own, y), ys, yr.at[y], (i, yb)).start()

    def wpart(m, n, h):
        return wf.at[m, pl.ds(mult(HID * up(n) + HALF * h, HALF), HALF), :]

    for m in range(3):
        for h in range(2):
            src = weights[m].at[pl.ds(HALF * h, HALF), :]
            remote(src, wpart(m, 0, h), ws.at[m, 0, h], wr.at[m, 0, h], (i, up(1))).start()
            back = weights[m].at[pl.ds(HALF * (1 - h), HALF), :]
            remote(back, wpart(m, 0, 1 - h), ws.at[m, 1, 1 - h], wr.at[m, 1, 1 - h], (i, up(-1))).start()
        pltpu.make_async_copy(
            weights[m], wf.at[m, pl.ds(mult(HID * y, HALF), HID), :], wl.at[m]
        ).start()

    def piece(s, f):
        return aux.at[s] if f == 4 else block(s, f)

    def zcopy(n, s, f, k):
        return remote(piece(s, f), piece(s, f), zs.at[(1 - n) // 2, k, f], zr.at[s, f], zdev(n))

    @pl.when(jnp.logical_and(column, jnp.logical_not(odd)))
    def _():
        block(s_own, y)[...] = stage[...]
        for d in range(1, NY):
            arrived(block(s_own, up(d)), yr.at[up(d)], ys)
        for f in (4, 0, 1, 2, 3):
            zcopy(1, s_own, f, 0).start()
            zcopy(-1, s_own, f, 0).start()
        s_a, s_b, s_c = zat(-2) // 2, zat(2) // 2, zat(4) // 2
        for f in (4, 0, 1, 2, 3):
            zcopy(1, s_a, f, 1).wait_recv()
            zcopy(1, s_a, f, 1).start()
            zcopy(-1, s_b, f, 1).wait_recv()
            zcopy(-1, s_b, f, 1).start()
        for f in (4, 0, 1, 2, 3):
            zcopy(1, s_c, f, 1).wait_recv()

    @pl.when(jnp.logical_and(column, odd))
    def _():
        s_a, s_b, s_c, s_d = zat(-1) // 2, zat(1) // 2, zat(-3) // 2, zat(3) // 2
        for f in (4, 0, 1, 2, 3):
            zcopy(1, s_a, f, 0).wait_recv()
            zcopy(1, s_a, f, 0).start()
            zcopy(-1, s_b, f, 0).wait_recv()
            zcopy(-1, s_b, f, 0).start()
        for f in (4, 0, 1, 2, 3):
            zcopy(1, s_c, f, 1).wait_recv()
            if f in (4, 0, 1):
                zcopy(1, s_c, f, 1).start()
            zcopy(1, s_d, f, 1).wait_recv()
            if f in (2, 3):
                zcopy(-1, s_d, f, 1).start()

    def rowpart(xsrc, pair):
        return rows.at[pl.ds(mult(2 * PAIR * xsrc + PAIR * pair, PAIR), PAIR), :]

    @pl.when(column)
    def _():
        for pair in range(2):
            slots = [aux[2 * pair + b, pl.ds(mult(8 * z, 8), 8), :] + float(CAP * b) for b in range(2)]
            gains = [aux[2 * pair + b, pl.ds(mult(EXPERTS + 8 * z, 8), 8), :] for b in range(2)]
            slots = jnp.concatenate(slots, axis=1)
            gains = jnp.concatenate(gains, axis=1)
            place = lax.broadcasted_iota(jnp.int32, (PAIR, 2 * TOK), 0).astype(F32)
            for j in range(8):
                chosen = place == slots[j : j + 1, :]
                smat[pair, PAIR * j : PAIR * (j + 1), :] = jnp.where(chosen, 1.0, 0.0).astype(BF16)
                gain = jnp.sum(jnp.where(chosen, gains[j : j + 1, :], 0.0), axis=1, keepdims=True)
                sendbuf[pair, PAIR * j : PAIR * (j + 1), 2 * D :] = jnp.broadcast_to(gain, (PAIR, 128)).astype(BF16)
            for f in range(NY):
                picked = dot_nn(smat[pair], blk[pair, f]).astype(BF16)
                sendbuf[pair, :, QD * f : QD * (f + 1)] = picked[:, 0:QD]
                sendbuf[pair, :, D + QD * f : D + QD * (f + 1)] = picked[:, QD:]
            for d in range(8):
                j = lax.rem(own + d, 8)
                src = sendbuf.at[pair, pl.ds(mult(PAIR * j, PAIR), PAIR), :]
                if d == 0:
                    pltpu.make_async_copy(src, rowpart(x, pair), xr.at[pair, x]).start()
                else:
                    remote(src, rowpart(x, pair), xs.at[pair, d], xr.at[pair, x], (8 * z + j, y)).start()

    for m in range(3):
        arrived(wpart(m, -1, 0), wr.at[m, 0, 0], ws.at[m, 0, 0])
        remote(wpart(m, -1, 0), wpart(m, -1, 0), ws.at[m, 0, 2], wr.at[m, 0, 2], (i, up(1))).start()
        arrived(wpart(m, 1, 1), wr.at[m, 1, 1], ws.at[m, 0, 0])
        remote(wpart(m, 1, 1), wpart(m, 1, 1), ws.at[m, 1, 2], wr.at[m, 1, 2], (i, up(-1))).start()

    def weight_whole(m):
        arrived(wpart(m, -1, 1), wr.at[m, 0, 1], ws.at[m, 0, 0])
        arrived(wpart(m, 1, 0), wr.at[m, 1, 0], ws.at[m, 0, 0])
        arrived(wpart(m, 2, 0), wr.at[m, 0, 2], ws.at[m, 0, 0])
        arrived(wpart(m, 2, 1), wr.at[m, 1, 2], ws.at[m, 0, 0])
        pltpu.make_async_copy(
            weights[m], wf.at[m, pl.ds(mult(HID * y, HALF), HID), :], wl.at[m]
        ).wait()

    for xsrc in range(NX):
        for pair in range(2):
            arrived(rowpart(xsrc, pair), xr.at[pair, xsrc], ys)

    weight = rows[:, 2 * D : 2 * D + 1].astype(F32)

    def gpart(m, n, h):
        return grad.at[m, pl.ds(mult(HID * up(n) + HALF * h, HALF), HALF), :]

    def grad_first(m):
        remote(gpart(m, 2, 0), rr.at[m, 0], gsend.at[m, 0], grecv.at[m, 0], (i, up(1))).start()
        remote(gpart(m, 2, 1), rr.at[m, 1], gsend.at[m, 1], grecv.at[m, 1], (i, up(-1))).start()
        remote(gpart(m, 1, 1), rr.at[m, 3], gsend.at[m, 3], grecv.at[m, 3], (i, up(1))).start()
        remote(gpart(m, -1, 0), rr.at[m, 5], gsend.at[m, 5], grecv.at[m, 5], (i, up(-1))).start()

    def grad_pass(m):
        for k, n, h, to in ((0, 1, 0, 1), (1, -1, 1, -1)):
            arrived(rr.at[m, k], grecv.at[m, k], ys)
            mine = gpart(m, n, h)
            mine[...] = (mine[...].astype(F32) + rr[m, k].astype(F32)).astype(BF16)
            remote(mine, rr.at[m, 2 + 2 * k], gsend.at[m, 2 + 2 * k], grecv.at[m, 2 + 2 * k], (i, up(to))).start()

    tiles = FF // 256

    def hidden(t):
        return pl.ds(mult(256 * t, 256), 256)

    def outer(m, left, at, t):
        turned = left.astype(F32).T.astype(BF16)
        for h in range(2):
            cols = slice(1024 * h, 1024 * (h + 1))
            grad[m, hidden(t), cols] = dot_nn(turned, rows[:, at + 1024 * h : at + 1024 * (h + 1)]).astype(BF16)

    weight_whole(0)
    weight_whole(1)

    @pl.loop(0, tiles)
    def _(t):
        g = dot_nt(rows[:, 0:D], wf[0, hidden(t), :])
        u = dot_nt(rows[:, 0:D], wf[1, hidden(t), :])
        gs[t] = g
        us[t] = u
        outer(2, (g * jax.nn.sigmoid(g) * u * weight).astype(BF16), D, t)

    grad_first(2)
    weight_whole(2)
    ap[...] = jnp.zeros_like(ap)

    @pl.loop(0, tiles)
    def _(t):
        g, u = gs[t], us[t]
        bh = dot_nt(rows[:, D : 2 * D], wf[2, hidden(t), :])
        sigma = jax.nn.sigmoid(g)
        active = g * sigma
        ap[...] += jnp.sum(active * u * bh, axis=1, keepdims=True)
        delta = bh * weight
        dg[t] = (delta * u * sigma * (1.0 + g * (1.0 - sigma))).astype(BF16)
        du[t] = (delta * active).astype(BF16)

    for h in range(2):
        cols = slice(1024 * h, 1024 * (h + 1))
        total = None
        for t in range(tiles):
            term = dot_nn(dg[t], wf[0, 256 * t : 256 * (t + 1), cols])
            term = term + dot_nn(du[t], wf[1, 256 * t : 256 * (t + 1), cols])
            total = term if total is None else total + term
        br[:, cols] = total.astype(BF16)
    score = ap[...]
    high = score.astype(BF16).astype(F32)
    low = score - high
    lane = lax.broadcasted_iota(jnp.int32, (ROWS, 128), 1)
    br[:, D:] = (jnp.where(lane == i, high, 0.0) + jnp.where(lane == i + EXPERTS, low, 0.0)).astype(BF16)

    def backpart(xsrc, pair):
        return br.at[pl.ds(mult(2 * PAIR * xsrc + PAIR * pair, PAIR), PAIR), :]

    def backslot(j, pair):
        return rb.at[pair, pl.ds(mult(PAIR * j, PAIR), PAIR), :]

    def back_send(d, pair):
        xsrc = lax.rem(x + d, NX)
        return remote(
            backpart(xsrc, pair), backslot(own, pair), bs.at[pair, d], brecv.at[pair, own],
            (8 * z + 2 * xsrc + y // 2, y),
        )

    def back_local(pair):
        return pltpu.make_async_copy(backpart(x, pair), backslot(own, pair), brecv.at[pair, own])

    for pair in range(2):
        for d in range(1, NX):
            back_send(d, pair).start()

        @pl.when(column)
        def _():
            back_local(pair).start()

        @pl.when(jnp.logical_not(column))
        def _():
            back_send(0, pair).start()

    @pl.loop(0, tiles)
    def _(t):
        outer(0, dg[t], 0, t)

    grad_first(0)

    @pl.loop(0, tiles)
    def _(t):
        outer(1, du[t], 0, t)

    grad_first(1)
    grad_pass(2)

    def plane(s):
        return part[s // 2, pl.ds(mult(TOK * lax.rem(s, 2), TOK), TOK), :]

    def zback(k, n, lanes=slice(None)):
        slot = k
        return remote(zt.at[k, :, lanes], zb.at[slot, :, lanes], zbs.at[k], zbr.at[slot], zdev(n))

    left, right = slice(0, 1024), slice(1024, BACK)

    @pl.when(column)
    def _():
        for pair in range(2):
            for j in range(8):
                arrived(backslot(j, pair), brecv.at[pair, j], ys)
            for cols in (slice(0, 1024), slice(1024, BACK)):
                part[pair, :, cols] = dot_tn(smat[pair], rb[pair, :, cols])

    @pl.when(jnp.logical_and(column, jnp.logical_not(odd)))
    def _():
        s_a, s_b, s_c = zat(-2) // 2, zat(2) // 2, zat(4) // 2
        far = plane(s_c).astype(BF16)
        zt[0] = far
        zt[1] = far
        zback(0, -1, left).start()
        zback(1, 1, right).start()
        zback(0, -1).wait_recv()
        zt[2] = (plane(s_a) + zb[0].astype(F32)).astype(BF16)
        zback(2, -1).start()
        zback(1, 1).wait_recv()
        zt[3] = (plane(s_b) + zb[1].astype(F32)).astype(BF16)
        zback(3, 1).start()
        zback(2, -1).wait_recv()
        zback(3, 1).wait_recv()
        fb[...] = (plane(s_own) + zb[2].astype(F32) + zb[3].astype(F32)).astype(BF16)
        zback(0, -1, left).wait_send()
        zback(1, 1, right).wait_send()
        zback(2, -1).wait_send()
        zback(3, 1).wait_send()

    @pl.when(jnp.logical_and(column, odd))
    def _():
        s_a, s_b, s_c, s_d = zat(-1) // 2, zat(1) // 2, zat(-3) // 2, zat(3) // 2
        zback(0, -1, left).wait_recv()
        zt[0, :, left] = (plane(s_c)[:, left] + zb[0, :, left].astype(F32)).astype(BF16)
        zt[0, :, right] = plane(s_c)[:, right].astype(BF16)
        zback(0, -1).start()
        zback(1, 1, right).wait_recv()
        zt[1, :, left] = plane(s_d)[:, left].astype(BF16)
        zt[1, :, right] = (plane(s_d)[:, right] + zb[1, :, right].astype(F32)).astype(BF16)
        zback(1, 1).start()
        zback(2, -1).wait_recv()
        zt[2] = (plane(s_a) + zb[2].astype(F32)).astype(BF16)
        zback(2, -1).start()
        zback(3, 1).wait_recv()
        zt[3] = (plane(s_b) + zb[3].astype(F32)).astype(BF16)
        zback(3, 1).start()
        for k, n in ((0, -1), (1, 1), (2, -1), (3, 1)):
            zback(k, n).wait_send()

    def last(d, k):
        to = up(d)
        if k == 0:
            src, dst = fb.at[:, pl.ds(mult(QD * to, QD), QD)], tg
        else:
            src, dst = fb.at[:, pl.ds(D, 128)], sc
        if d == 0:
            return pltpu.make_async_copy(src, dst, lr.at[k])
        return remote(src, dst, ls.at[k, d], lr.at[k], (i, to))

    @pl.when(owner)
    def _():
        for d in range(NY):
            for k in range(2):
                last(d, k).start()

    grad_pass(0)
    grad_pass(1)

    for m in (2, 0, 1):
        for h, near, far in ((0, 5, 2), (1, 3, 4)):
            arrived(rr.at[m, near], grecv.at[m, near], ys)
            arrived(rr.at[m, far], grecv.at[m, far], ys)
            fin[h] = gpart(m, 0, h)[...].astype(F32) + (rr[m, near].astype(F32) + rr[m, far].astype(F32))
            sums_ref[m, HALF * h : HALF * (h + 1), :] = fin[h].astype(sums_ref.dtype)

    arrived(tg, lr.at[0], ys)
    arrived(sc, lr.at[1], ys)
    tgrad_ref[...] = tg[...]
    known = sc[:, 0:EXPERTS].astype(F32) + sc[:, EXPERTS:].astype(F32)
    expert = lax.broadcasted_iota(jnp.int32, (TOK, EXPERTS), 1)
    for k in range(8):
        same = expert == routes_ref[:, k : k + 1]
        rgrad_ref[:, k : k + 1] = jnp.sum(jnp.where(same, known, 0.0), axis=1, keepdims=True)

    @pl.when(jnp.logical_not(owner))
    def _():
        sent(stage, ys, yr.at[0])

    @pl.when(owner)
    def _():
        for d in range(1, NY):
            for k in range(2):
                last(d, k).wait_send()

    for m in range(3):
        for n in range(2):
            for k in range(3):
                sent(wpart(m, 0, 0), ws.at[m, n, k], wr.at[m, 0, 0])
        for k in range(6):
            sent(rr.at[m, k], gsend.at[m, k], grecv.at[m, k])

    @pl.when(jnp.logical_and(column, jnp.logical_not(odd)))
    def _():
        for f in range(5):
            for k in range(2):
                for n in (1, -1):
                    zcopy(n, s_own, f, k).wait_send()

    @pl.when(jnp.logical_and(column, odd))
    def _():
        for f in range(5):
            for n in (1, -1):
                zcopy(n, s_own, f, 0).wait_send()
            zcopy(1 if f in (4, 0, 1) else -1, s_own, f, 1).wait_send()

    @pl.when(column)
    def _():
        for pair in range(2):
            for d in range(1, 8):
                sent(rowpart(0, 0), xs.at[pair, d], xr.at[0, 0])

    for pair in range(2):
        for d in range(1, NX):
            back_send(d, pair).wait_send()

        @pl.when(jnp.logical_not(column))
        def _():
            back_send(0, pair).wait_send()


def exchange(tokens, cotangent, routes_t, gains_t, routes, w_gate, w_up, w_down):
    vmem = pl.BlockSpec(memory_space=pltpu.VMEM)
    whole = pl.BlockSpec(memory_space=pl.ANY)
    dma = pltpu.SemaphoreType.DMA
    return pl.pallas_call(
        kernel,
        out_shape=(
            jax.ShapeDtypeStruct((3, HID, D), BF16),
            jax.ShapeDtypeStruct((TOK, QD), BF16),
            jax.ShapeDtypeStruct((TOK, 8), F32),
        ),
        in_specs=[vmem] * 5 + [whole] * 3,
        out_specs=(vmem, vmem, vmem),
        scratch_shapes=[
            pltpu.VMEM((3, FF, D), BF16),
            pltpu.VMEM((3, FF, D), BF16),
            pltpu.VMEM((3, 6, HALF, D), BF16),
            pltpu.VMEM((2, NY, 2 * TOK, 2 * QD), BF16),
            pltpu.VMEM((4, 2 * EXPERTS, TOK), F32),
            pltpu.VMEM((2, 8 * PAIR, WIDE), BF16),
            pltpu.VMEM((ROWS, WIDE), BF16),
            pltpu.VMEM((2, 8 * PAIR, 2 * TOK), BF16),
            pltpu.VMEM((3, ROWS, 256), F32),
            pltpu.VMEM((3, ROWS, 256), F32),
            pltpu.VMEM((ROWS, 1), F32),
            pltpu.VMEM((3, ROWS, 256), BF16),
            pltpu.VMEM((3, ROWS, 256), BF16),
            pltpu.VMEM((ROWS, BACK), BF16),
            pltpu.VMEM((2, 8 * PAIR, BACK), BF16),
            pltpu.VMEM((2, 2 * TOK, BACK), F32),
            pltpu.VMEM((4, TOK, BACK), BF16),
            pltpu.VMEM((4, TOK, BACK), BF16),
            pltpu.VMEM((TOK, BACK), BF16),
            pltpu.VMEM((TOK, 2 * QD), BF16),
            pltpu.VMEM((TOK, QD), BF16),
            pltpu.VMEM((TOK, 128), BF16),
            pltpu.VMEM((2, HALF, D), F32),
            dma((3, 2, 3)),
            dma((3, 2, 3)),
            dma((3,)),
            dma((3, 6)),
            dma((3, 6)),
            dma,
            dma((NY,)),
            dma((2, 2, 5)),
            dma((4, 5)),
            dma((2, 8)),
            dma((2, NX)),
            dma((2, NX)),
            dma((2, 8)),
            dma((4,)),
            dma((4,)),
            dma((2, NY)),
            dma((2,)),
        ],
        compiler_params=pltpu.CompilerParams(
            collective_id=0, has_side_effects=True, vmem_limit_bytes=64 * 1024 * 1024 - 256 * 1024
        ),
    )(tokens, cotangent, routes_t, gains_t, routes, w_gate, w_up, w_down)


def soften(grid, latent, scale):
    level = grid.astype(F32) + 0.5 * (1.0 + jnp.tanh(latent.astype(F32) / temper))
    return (level * scale).astype(BF16)


def latent_grad(grad_weight, latent, scale):
    slope = jnp.tanh(latent.astype(F32) / temper)
    return (grad_factor * grad_weight.astype(F32) * scale * (1.0 - slope * slope) / (2.0 * temper))[None]


def body(
    tokens, cotangent, route_weights, routes,
    grid_gate, latent_gate, scale_gate,
    grid_up, latent_up, scale_up,
    grid_down, latent_down, scale_down,
):
    rows_g, rows_u, cols_d = scale_gate[0][:, None], scale_up[0][:, None], scale_down[0][None, :]
    sums, token_grad, route_grad = exchange(
        tokens, cotangent, routes.T, route_weights.astype(F32).T, routes,
        soften(grid_gate[0], latent_gate[0], rows_g),
        soften(grid_up[0], latent_up[0], rows_u),
        soften(grid_down[0], latent_down[0], cols_d),
    )
    return (
        latent_grad(sums[0], latent_gate[0], rows_g),
        latent_grad(sums[1], latent_up[0], rows_u),
        latent_grad(sums[2], latent_down[0], cols_d),
        token_grad,
        route_grad,
    )


def solution(mesh):
    return jax.shard_map(
        body,
        mesh=mesh,
        in_specs=(
            P("ep", "tp"), P("ep", "tp"), P("ep", None), P("ep", None),
            P("ep", "tp", None), P("ep", "tp", None), P("ep", "tp"),
            P("ep", "tp", None), P("ep", "tp", None), P("ep", "tp"),
            P("ep", "tp", None), P("ep", "tp", None), P("ep", None),
        ),
        out_specs=(
            P("ep", "tp", None), P("ep", "tp", None), P("ep", "tp", None), P("ep", "tp"), P("ep", None),
        ),
        check_vma=False,
    )
```

time: 511 us -> 198 us (0.39)
  waiting for transfers between devices: 254 us -> 0 us
  Pallas kernels: 0 us -> 176 us
  blocking collectives: 119 us -> 0 us
  local copies, waits for them, and re-layouts: 50 us -> 3.6 us
  matrix products: 33.1 us -> 0 us
  between operations: 14.5 us -> 0.7 us
  other arithmetic: 27.3 us -> 14.2 us
  starting transfers between devices: 10.7 us -> 0 us
    pallas_call x0 -> x1, Pallas kernels: none -> 176 us  [exchange(): pl.pallas_call(kernel, out_shape=(jax.ShapeDtypeStruct((3, HID, D), BF16)...]
    all_to_all x3 -> x0, blocking collectives: 119 us -> none  [the longest x1 92.6 us: sent_together(): lax.all_to_all(both, axis, split_axis=split_dim, concat_axis=concat_dim,...]
    all_gather x1 -> x0, waiting for transfers between devices: 117 us -> none  [side_by_side(): lax.all_gather(both, axis, axis=dim, tiled=True)]
    reduce_scatter x1 -> x0, waiting for transfers between devices: 90 us -> none  [body(): share = lax.psum_scatter(back_rows, 'tp', scatter_dimension=2, tiled=True)]
    all_to_all x1 -> x0, waiting for transfers between devices: 47.4 us -> none  [body(): lax.all_to_all(share, 'ep', split_axis=0, concat_axis=0, tiled=True)]
    dot_general x8 -> x0, matrix products: 33.1 us -> none  [the longest x1 6.59 us: expert_backward(): jnp.dot(grad_upper, w_up, preferred_element_type=jnp.float32)]
    gather x5 -> x0, local copies, waits for them, and re-layouts: 30.1 us -> none  [the longest x1 9.46 us: body(): send_weights = weights_pad[table].reshape(experts, capacity)]
    another operation x3 -> x0, other arithmetic: 18.2 us -> none
  transfers between devices with their start and end apart: 3 -> 0, of which waited for: 3 -> 0; matrix products, arithmetic and copies ran while one was open for 6% -> 0% of each run, Pallas kernels for 0% -> 0%
where the time goes in v1:
time: 198 us; the launch traced here: 194 us
  Pallas kernels  176 us (89%)
  other arithmetic  14.2 us (7%)
  local copies, waits for them, and re-layouts  3.6 us (2%)
    pallas_call x1, Pallas kernels, exchange(): pl.pallas_call(kernel, out_shape=(jax.ShapeDtypeStruct((3, HID, D), BF16)...  176 us
    convert_element_type x2, other arithmetic, soften(): return (level * scale).astype(BF16)  5.93 us
    div x1, other arithmetic, latent_grad(): grad_factor * grad_weight.astype(F32) * scale * (1.0 - slope * slope)  5.43 us

profile of v1, /device:TPU:38, one launch (start us, length us, event | category | flops | bytes accessed | tf_op | source)
XLA Modules:
  0.0 194.1 jit_solution(277232900102010675)
XLA Ops:
  0.6 0.0 copy-start
  0.6 0.0 copy-start.1
  0.7 0.0 copy-start.4
  0.7 0.0 copy-start.2
  0.7 0.0 copy-start.5
  0.7 0.8 broadcast_multiply_fusion.1
  1.5 1.3 convert_bitcast_fusion.wt_ref
  2.8 0.7 broadcast_multiply_fusion
  3.5 1.4 copy.18.routes_ref
  4.9 2.8 %fusion.2.wg_ref = bf16[192,2048]{1,0:T(8,128)(2,1)} fusion(bf16[1,192,2048]{2,1,0:T(8,128)(2,1)} %param.17, bf16[1,192,2048]{2,1,0:T(8,128)(2,1)} %param.18, f32[192]{0:T(256)} %bitcast.22), kind=kLoop, calls=%fused_computation.5 | loop fusion | flops 3145728 | bytes 2360064 | tf_op jit(solution)/shard_map/convert_element_type | solution.py:522
  7.7 0.0 copy-done
  7.7 0.0 copy-done.1
  7.7 0.0 copy-done.4
  7.7 0.0 copy-done.2
  7.7 0.0 copy-done.5
  7.7 3.2 %fusion = (bf16[192,2048]{1,0:T(8,128)(2,1)}, bf16[192,2048]{1,0:T(8,128)(2,1)}) fusion(bf16[1,192,2048]{2,1,0:T(8,128)(2,1)S(1)} %copy-done.2, bf16[1,192,2048]{2,1,0:T(8,128)(2,1)S(1)} %copy-done, f32[2048]{0:T(1024)S(1)} %bitcast.19, f32[192]{0:T(256)S(1)} %bitcast.24, bf16[1,192,2048]{2,1,0:T(8,128)(2,1)S(1)} %copy-done.1, bf16[1,192,2048]{2,1,0:T(8,128)(2,1)} %param.20), kind=kLoop, calls=%fused_computation.1 | loop fusion | flops 6291456 | bytes 4727552 | tf_op jit(solution)/shard_map/convert_element_type | solution.py:522
  10.9 175.7 %shard_map.164 = (bf16[3,192,2048]{2,1,0:T(8,128)(2,1)}, bf16[128,512]{1,0:T(8,128)(2,1)}, f32[128,8]{1,0:T(8,128)}) custom-call(bf16[128,512]{1,0:T(8,128)(2,1)} %tok_ref.1, bf16[128,512]{1,0:T(8,128)(2,1)} %cot_ref.1, s32[8,128]{1,0:T(8,128)} %bitcast.20, f32[8,128]{1,0:T(8,128)} %convert_bitcast_fusion.wt_ref, s32[128,8]{1,0:T(8,128)} %copy.18.routes_ref, ...), custom_call_target="tpu_custom_call" | custom-call | tf_op jit(solution)/shard_map/pallas_call | solution.py:463
  186.5 1.5 copy.19
  188.1 0.0 copy-start.3
  188.1 5.4 %multiply_multiply_fusion = (f32[1,192,2048]{2,1,0:T(8,128)}, f32[1,192,2048]{2,1,0:T(8,128)}, f32[1,192,2048]{2,1,0:T(8,128)}) fusion(bf16[1,192,2048]{2,1,0:T(8,128)(2,1)} %param.24, f32[2048]{0:T(1024)S(1)} %broadcast_multiply_fusion, bf16[3,192,2048]{2,1,0:T(8,128)(2,1)} %get-tuple-element.8, bf16[1,192,2048]{2,1,0:T(8,128)(2,1)} %param.21, ...), kind=kLoop, calls=%fused_computation.6 | loop fusion | flops 9437184 | bytes 9446912 | tf_op jit(solution)/shard_map/div | solution.py:527
  193.5 0.0 copy-done.3
  193.5 0.7 copy.21
Async XLA Ops:
  0.6 7.1 %copy-start = (bf16[1,192,2048]{2,1,0:T(8,128)(2,1)S(1)}, bf16[1,192,2048]{2,1,0:T(8,128)(2,1)}, u32[]{:S(2)}) copy-start(bf16[1,192,2048]{2,1,0:T(8,128)(2,1)} %param.24) | copy-start | bytes 2359300
  0.6 7.1 %copy-start.1 = (bf16[1,192,2048]{2,1,0:T(8,128)(2,1)S(1)}, bf16[1,192,2048]{2,1,0:T(8,128)(2,1)}, u32[]{:S(2)}) copy-start(bf16[1,192,2048]{2,1,0:T(8,128)(2,1)} %param.21) | copy-start | bytes 2359300
  0.7 7.0 %copy-start.4 = (f32[1,2048]{1,0:T(1,128)S(1)}, f32[1,2048]{1,0:T(1,128)}, u32[]{:S(2)}) copy-start(f32[1,2048]{1,0:T(1,128)} %param.25) | copy-start | bytes 24580
  0.7 7.0 %copy-start.2 = (bf16[1,192,2048]{2,1,0:T(8,128)(2,1)S(1)}, bf16[1,192,2048]{2,1,0:T(8,128)(2,1)}, u32[]{:S(2)}) copy-start(bf16[1,192,2048]{2,1,0:T(8,128)(2,1)} %param.23) | copy-start | bytes 2359300
  0.7 7.0 %copy-start.5 = (f32[1,192]{1,0:T(1,128)S(1)}, f32[1,192]{1,0:T(1,128)}, u32[]{:S(2)}) copy-start(f32[1,192]{1,0:T(1,128)} %param.22) | copy-start | bytes 2308
  188.1 5.4 %copy-start.3 = (bf16[128,512]{1,0:T(8,128)(2,1)S(1)}, bf16[128,512]{1,0:T(8,128)(2,1)}, u32[]{:S(2)}) copy-start(bf16[128,512]{1,0:T(8,128)(2,1)} %get-tuple-element.31) | copy-start | bytes 393220

commit v2 on v0

v2 whole, which is shorter than its diff:
```python
import jax
import jax.numpy as jnp
from jax import lax
from jax.experimental import pallas as pl
from jax.experimental.pallas import tpu as pltpu
from jax.sharding import PartitionSpec as P

temper = 0.25
grad_factor = 8.0

NZ, NX, NY = 8, 4, 4
D, FF, TOK, EXPERTS, CAP = 2048, 768, 128, 64, 24
QD = D // NY
HID = FF // NY
HH = 2 * HID
SRC = 4 * CAP
ROWS = NX * SRC
EXTRA = 128
F32, BF16 = jnp.float32, jnp.bfloat16
MESH = pl.DeviceIdType.MESH


def dot_nt(a, b):
    return lax.dot_general(a, b, (((1,), (1,)), ((), ())), preferred_element_type=F32)


def dot_nn(a, b):
    return lax.dot_general(a, b, (((1,), (0,)), ((), ())), preferred_element_type=F32)


ORDER = (0, 1, 3, 2)


def going(f, h):
    at = EXTRA + 2 * QD * f + QD * h
    return slice(at, at + QD)


def lanes_of(f):
    return pl.ds(pl.multiple_of(EXTRA + 2 * QD * f, 128), 2 * QD)


def coming(f):
    return slice(QD * f, QD * (f + 1) + (EXTRA if f == NY - 1 else 0))


def feature(f):
    return slice(QD * f, QD * (f + 1))


def kernel(
    tok_ref, cot_ref, rt_ref, wt_ref, gg_ref, lg_ref, gu_ref, lu_ref, gd_ref, ld_ref, sg_ref, su_ref, sd_ref,
    og_ref, ou_ref, od_ref, tgrad_ref, rgrad_ref,
    raw, wf, grad, rr, blk, aux, sendbuf, rows, smat, smt, gs, us, bh, sco, dg, du, lt,
    bown, bsend, bgot, br, rb, part, zb, zt, fb, stage, tg, sc,
    rawsem, ws, wr, gsend, grecv, ys, yr, zs, zr, xs, xr, fs, fr, es, er, bs, brr, zbs, zbr, ls, lr,
):
    i, y = lax.axis_index("ep"), lax.axis_index("tp")
    z, x, c = i // 8, lax.rem(i, 8) // 2, lax.rem(i, 2)
    own = 2 * x + c
    column = c == y // 2
    odd = lax.rem(z + y, 2) == 1
    source = jnp.logical_and(column, jnp.logical_not(odd))
    relay = jnp.logical_and(column, odd)
    yb = 2 * c + lax.rem(z, 2)
    owner = y == yb
    flip, mirror = y + 1 - 2 * lax.rem(y, 2), NY - 1 - y
    wpair = flip * (1 - c) + mirror * c
    rpair = mirror * (1 - c) + flip * c

    def up(n):
        return lax.rem(y + n + NY, NY)

    def zat(n):
        return lax.rem(z + n + NZ, NZ)

    def zdev(n):
        return (8 * zat(n) + own, y)

    def remote(src, dst, send, recv, dev):
        return pltpu.make_async_remote_copy(
            src_ref=src, dst_ref=dst, send_sem=send, recv_sem=recv, device_id=dev, device_id_type=MESH
        )

    def arrived(dst, recv):
        remote(dst, dst, ys, recv, (i, up(1))).wait_recv()

    def sent(src, send):
        remote(src, src, send, yr.at[0], (i, up(1))).wait_send()

    raws = ((gg_ref, lg_ref), (gu_ref, lu_ref), (gd_ref, ld_ref))
    for m in range(3):
        for k in range(2):
            pltpu.make_async_copy(raws[m][k], raw.at[m, k], rawsem.at[m, k]).start()

    barrier = pltpu.get_barrier_semaphore()
    for d in range(1, NY):
        pl.semaphore_signal(barrier, inc=1, device_id=(i, up(d)), device_id_type=MESH)
    for d in (1, -1, 2, -2, 3, -3):
        pl.semaphore_signal(barrier, inc=1, device_id=zdev(d), device_id_type=MESH)
    for d in range(1, 8):
        pl.semaphore_signal(barrier, inc=1, device_id=(8 * z + lax.rem(own + d, 8), y), device_id_type=MESH)

    stage[:, 0:QD] = tok_ref[...]
    stage[:, QD:] = cot_ref[...]
    s_own = z // 2
    order = [up(d) for d in ORDER]

    def block(s, f):
        return blk.at[f, pl.ds(pl.multiple_of(TOK * s, TOK), TOK), :]

    @pl.when(owner)
    def _():
        expert = lax.broadcasted_iota(jnp.int32, (EXPERTS, TOK), 0)
        hit = jnp.zeros((EXPERTS, TOK), F32)
        weight = jnp.zeros((EXPERTS, TOK), F32)
        gains = wt_ref[...].astype(F32)
        for k in range(8):
            same = expert == rt_ref[k : k + 1, :]
            hit = hit + jnp.where(same, 1.0, 0.0)
            weight = weight + jnp.where(same, gains[k : k + 1, :], 0.0)
        before = lax.broadcasted_iota(jnp.int32, (TOK, TOK), 0) < lax.broadcasted_iota(jnp.int32, (TOK, TOK), 1)
        slot = dot_nn(hit.astype(BF16), jnp.where(before, 1.0, 0.0).astype(BF16))
        aux[s_own, 0:EXPERTS, :] = jnp.where(hit > 0.0, slot, -1000.0)
        aux[s_own, EXPERTS:, :] = weight

    pl.semaphore_wait(barrier, 3 + 6 + 7)

    @pl.when(jnp.logical_not(owner))
    def _():
        remote(stage, block(s_own, y), ys, yr.at[y], (i, yb)).start()

    def piece(s, f):
        return aux.at[s] if f is None else block(s, f)

    def zcopy(n, s, f):
        at = 4 if f is None else f
        return remote(piece(s, f), piece(s, f), zs.at[int(n < 0), abs(n) - 1, at], zr.at[s, at], zdev(n))

    def zgot(s, f):
        arrived(piece(s, f), zr.at[s, 4 if f is None else f])

    def give(f):
        zcopy(1, s_own, f).start()
        zcopy(-1, s_own, f).start()

    def both(k):
        return (None, order[0]) if k == 0 else (order[k],)

    @pl.when(source)
    def _():
        block(s_own, y)[...] = stage[...]
        give(None)
        give(y)

    diagonal = lax.broadcasted_iota(jnp.int32, (HID, HID), 0) == lax.broadcasted_iota(jnp.int32, (HID, HID), 1)

    def column_of(ref):
        return jnp.sum(jnp.where(diagonal, ref[...], 0.0), axis=1, keepdims=True)

    sco[0, 0:HID, :] = column_of(sg_ref)
    sco[1, 0:HID, :] = column_of(su_ref)

    def scale_of(m, at, n):
        return sd_ref[...] if m == 2 else sco[m, pl.ds(at, n), :]

    def wcopy(m):
        return remote(wf.at[m, 0:HID, :], wf.at[m, HID:HH, :], ws.at[m], wr.at[m], (i, wpair))

    def soften(m):
        for k in range(2):
            pltpu.make_async_copy(raws[m][k], raw.at[m, k], rawsem.at[m, k]).wait()

        @pl.loop(0, HID // 16)
        def _(t):
            at = pl.multiple_of(16 * t, 16)
            grid = raw[m, 0, pl.ds(at, 16), :].astype(F32)
            latent = raw[m, 1, pl.ds(at, 16), :].astype(F32)
            level = grid + 0.5 * (1.0 + jnp.tanh(latent / temper))
            wf[m, pl.ds(at, 16), :] = (level * scale_of(m, at, 16)).astype(BF16)

        wcopy(m).start()

    soften(0)
    soften(1)
    soften(2)

    @pl.when(source)
    def _():
        for f in order[1:]:
            arrived(block(s_own, f), yr.at[f])
            give(f)

    def relay_piece(k):
        for f in both(k):
            zgot(zat(-1) // 2, f)
            zcopy(1, zat(-1) // 2, f).start()
            zcopy(2, zat(-1) // 2, f).start()
            if k < 2:
                zcopy(3, zat(-1) // 2, f).start()
            zgot(zat(1) // 2, f)
            zcopy(-1, zat(1) // 2, f).start()
            zcopy(-2, zat(1) // 2, f).start()
            if k >= 2:
                zcopy(-3, zat(1) // 2, f).start()

    @pl.when(relay)
    def _():
        relay_piece(0)
        relay_piece(1)

    def rowpart(xsrc, lanes):
        return rows.at[pl.ds(pl.multiple_of(SRC * xsrc, SRC), SRC), lanes]

    def out_lanes(k):
        return slice(0, EXTRA) if k == NY else lanes_of(order[k])

    def row_send(d, k):
        j = lax.rem(own + d, 8)
        src = sendbuf.at[pl.ds(pl.multiple_of(SRC * j, SRC), SRC), out_lanes(k)]
        if d == 0:
            return pltpu.make_async_copy(src, rowpart(x, out_lanes(k)), xr.at[k, x])
        return remote(src, rowpart(x, out_lanes(k)), xs.at[k, d], xr.at[k, x], (8 * z + j, y))

    def swap_rows(k):
        return remote(
            rows.at[0:ROWS, out_lanes(k)], rows.at[ROWS : 2 * ROWS, out_lanes(k)], fs.at[k], fr.at[k], (i, rpair)
        )

    def with_extra(k):
        return (NY, 0) if k == 0 else (k,)

    def forward(k):
        for g in with_extra(k):
            for xsrc in range(NX):
                arrived(rowpart(xsrc, out_lanes(g)), xr.at[g, xsrc])
            swap_rows(g).start()

    for k in range(NY):

        @pl.when(source)
        def _():
            for f in both(k):
                for n in (2, -2, 4):
                    zgot(zat(n) // 2, f)

        @pl.when(relay)
        def _():
            for f in both(k):
                for n in (3, -3):
                    zgot(zat(n) // 2, f)

        @pl.when(column)
        def _():
            if k == 0:
                slots = [aux[s, pl.ds(pl.multiple_of(8 * z, 8), 8), :] + float(CAP * s) for s in range(4)]
                gains = [aux[s, pl.ds(pl.multiple_of(EXPERTS + 8 * z, 8), 8), :] for s in range(4)]
                slots, gains = jnp.concatenate(slots, axis=1), jnp.concatenate(gains, axis=1)
                place = lax.broadcasted_iota(jnp.int32, (SRC, 4 * TOK), 0).astype(F32)
                for j in range(8):
                    chosen = place == slots[j : j + 1, :]
                    smat[SRC * j : SRC * (j + 1), :] = jnp.where(chosen, 1.0, 0.0).astype(BF16)
                    gain = jnp.sum(jnp.where(chosen, gains[j : j + 1, :], 0.0), axis=1, keepdims=True)
                    sendbuf[SRC * j : SRC * (j + 1), 0:EXTRA] = jnp.broadcast_to(gain, (SRC, EXTRA)).astype(BF16)
            f = order[k]
            for h in range(2):
                picked = dot_nn(smat[...], blk[f, :, QD * h : QD * (h + 1)])
                sendbuf[:, pl.ds(pl.multiple_of(EXTRA + 2 * QD * f + QD * h, 128), QD)] = picked.astype(BF16)
            for g in with_extra(k):
                for d in range(8):
                    row_send(d, g).start()

        @pl.when(relay)
        def _():
            if k + 2 < NY:
                relay_piece(k + 2)

        if k >= 1:
            forward(k - 1)
    forward(NY - 1)

    @pl.when(column)
    def _():
        for t in range(4):
            lanes = slice(TOK * t, TOK * (t + 1))
            smt[lanes, :] = smat[:, lanes].astype(F32).T.astype(BF16)

    for m in range(3):
        wcopy(m).wait_recv()

    def hidden(r):
        part_rows = slice(ROWS * r, ROWS * (r + 1))
        for out, m, h in ((gs, 0, 0), (us, 1, 0), (bh, 2, 1)):
            total = None
            for f in range(NY):
                term = dot_nt(rows[part_rows, going(f, h)], wf[m, :, feature(f)])
                total = term if total is None else total + term
            out[...] = total

        @pl.loop(0, ROWS // 128)
        def _(t):
            at = pl.multiple_of(128 * t, 128)
            here = pl.ds(at, 128)
            g, u, back = gs[here, :], us[here, :], bh[here, :]
            weight = rows[pl.ds(pl.multiple_of(ROWS * r + at, 128), 128), 0:EXTRA][:, 0:1].astype(F32)
            sigma = jax.nn.sigmoid(g)
            active = g * sigma
            value = active * u
            score = jnp.sum(value * back, axis=1, keepdims=True)
            delta = back * weight
            there = pl.ds(pl.multiple_of(ROWS * r + at, 128), 128)
            d_gate = delta * u * sigma * (1.0 + g * (1.0 - sigma))
            d_up = delta * active
            dg[here, :] = d_gate.astype(BF16)
            du[here, :] = d_up.astype(BF16)
            sco[2 + r, here, :] = score
            lt[0, :, there] = d_gate.T.astype(BF16)
            lt[1, :, there] = d_up.T.astype(BF16)
            lt[2, :, there] = (value * weight).T.astype(BF16)

    def back_of(f):
        return dot_nn(dg[...], wf[0, :, feature(f)]) + dot_nn(du[...], wf[1, :, feature(f)])

    lane = lax.broadcasted_iota(jnp.int32, (ROWS, EXTRA), 1)

    def split(score):
        high = score.astype(BF16).astype(F32)
        spread = jnp.where(lane == i, high, 0.0) + jnp.where(lane == i + EXPERTS, score - high, 0.0)
        return spread.astype(BF16)

    def swap_back(f):
        return remote(bsend.at[:, coming(f)], bgot.at[:, coming(f)], es.at[f], er.at[f], (i, rpair))

    hidden(0)
    for f in range(NY):
        bown[:, feature(f)] = back_of(f)
    for k in range(NY + 1):
        lanes = slice(0, EXTRA) if k == NY else lanes_of(lax.rem(rpair + ORDER[k], NY))
        arrived(rows.at[ROWS : 2 * ROWS, lanes], fr.at[k])
    hidden(1)
    for f in range(NY):
        bsend[:, feature(f)] = back_of(f).astype(BF16)
        if f == NY - 1:
            score = sco[3, :, :]
            high = score.astype(BF16).astype(F32)
            spread = jnp.where(lane == 0, high, 0.0) + jnp.where(lane == 1, score - high, 0.0)
            bsend[:, D:] = spread.astype(BF16)
        swap_back(f).start()

    def gcopy(m):
        return remote(grad.at[m, HID:HH, :], rr.at[m], gsend.at[m], grecv.at[m], (i, wpair))

    def outer(m):
        h = 1 if m == 2 else 0
        for f in range(NY):
            grad[m, :, feature(f)] = dot_nn(lt[m], rows[:, going(f, h)]).astype(BF16)

    def back_send(d, f):
        xsrc = lax.rem(x + d, NX)
        return remote(
            br.at[pl.ds(pl.multiple_of(SRC * xsrc, SRC), SRC), coming(f)],
            rb.at[pl.ds(pl.multiple_of(SRC * own, SRC), SRC), coming(f)],
            bs.at[f, d], brr.at[f, own], (8 * z + 2 * xsrc + y // 2, y),
        )

    def give_back(f):
        swap_back(f).wait_recv()
        br[:, feature(f)] = (bown[:, feature(f)] + bgot[:, feature(f)].astype(F32)).astype(BF16)
        if f == NY - 1:
            other = bgot[:, D:].astype(F32)
            br[:, D:] = split(sco[2, :, :] + (other[:, 0:1] + other[:, 1:2]))
        for d in range(1, NX):
            back_send(d, f).start()

        @pl.when(column)
        def _():
            pltpu.make_async_copy(
                br.at[pl.ds(pl.multiple_of(SRC * x, SRC), SRC), coming(f)],
                rb.at[pl.ds(pl.multiple_of(SRC * own, SRC), SRC), coming(f)], brr.at[f, own],
            ).start()

        @pl.when(jnp.logical_not(column))
        def _():
            back_send(0, f).start()

    def plane(s, f):
        return part.at[pl.ds(pl.multiple_of(TOK * s, TOK), TOK), coming(f)]

    def zback(src, n, slot, f):
        return remote(src, zb.at[slot, :, coming(f)], zbs.at[f, slot], zbr.at[f, slot], zdev(n))

    def got(slot, f):
        arrived(zb.at[slot, :, coming(f)], zbr.at[f, slot])
        return zb[slot, :, coming(f)].astype(F32)

    def mine(n, f):
        return plane(zat(n) // 2, f)

    def combine(f):
        for j in range(8):
            arrived(rb.at[pl.ds(SRC * j, SRC), coming(f)], brr.at[f, j])
        part[:, coming(f)] = dot_nn(smt[...], rb[:, coming(f)]).astype(BF16)

    def last(f):
        @pl.when(y == f)
        def _():
            pltpu.make_async_copy(fb.at[:, feature(f)], tg, lr.at[0]).start()

        @pl.when(y != f)
        def _():
            remote(fb.at[:, feature(f)], tg, ls.at[f], lr.at[0], (i, f)).start()

    def last_score(d):
        src = fb.at[:, D:]
        if d == 0:
            return pltpu.make_async_copy(src, sc, lr.at[1])
        return remote(src, sc, ls.at[NY + d], lr.at[1], (i, up(d)))

    def one(f):
        @pl.when(column)
        def _():
            combine(f)

        @pl.when(source)
        def _():
            zback(mine(-2, f), -1, 0, f).start()
            zback(mine(2, f), 1, 1, f).start()
            zback(mine(4, f), -3 if f < 2 else 3, 4, f).start()

        @pl.when(relay)
        def _():
            zback(mine(-3, f), -2, 2, f).start()
            zback(mine(3, f), 2, 3, f).start()

    def two(f):
        @pl.when(relay)
        def _():
            for side, n in ((0, -1), (1, 1)):
                total = mine(n, f)[...].astype(F32) + (got(side, f) + got(2 + side, f))
                if (f < 2) == (side == 0):
                    total = total + got(4, f)
                zt[side, :, coming(f)] = total.astype(BF16)
                zback(zt.at[side, :, coming(f)], n, side, f).start()

    def three(f):
        @pl.when(source)
        def _():
            fb[:, coming(f)] = (mine(0, f)[...].astype(F32) + (got(0, f) + got(1, f))).astype(BF16)
            last(f)
            if f == NY - 1:
                for d in range(NY):
                    last_score(d).start()

    outer(2)
    give_back(0)
    outer(0)
    give_back(1)
    one(0)
    outer(1)
    give_back(2)
    one(1)
    two(0)
    give_back(3)
    for m in (2, 0, 1):
        gcopy(m).start()
    one(2)
    two(1)
    three(0)
    one(3)
    two(2)
    three(1)
    two(3)
    three(2)
    three(3)

    def finish(m, out):
        gcopy(m).wait_recv()

        @pl.loop(0, HID // 16)
        def _(t):
            at = pl.multiple_of(16 * t, 16)
            here = pl.ds(at, 16)
            slope = jnp.tanh(raw[m, 1, here, :].astype(F32) / temper)
            total = grad[m, here, :].astype(F32) + rr[m, here, :].astype(F32)
            value = grad_factor * total * scale_of(m, at, 16) * (1.0 - slope * slope) / (2.0 * temper)
            out[here, :] = value.astype(BF16)

    finish(2, od_ref)
    finish(0, og_ref)
    finish(1, ou_ref)

    arrived(tg, lr.at[0])
    arrived(sc, lr.at[1])
    tgrad_ref[...] = tg[...]
    turned = sc[...].astype(F32).T
    known = turned[0:EXPERTS, :] + turned[EXPERTS:, :]
    expert = lax.broadcasted_iota(jnp.int32, (EXPERTS, TOK), 0)
    for k in range(8):
        same = expert == rt_ref[k : k + 1, :]
        rgrad_ref[k : k + 1, :] = jnp.sum(jnp.where(same, known, 0.0), axis=0, keepdims=True)

    @pl.when(jnp.logical_not(owner))
    def _():
        sent(stage, ys)

    @pl.when(owner)
    def _():
        for d in range(1, NY):
            last_score(d).wait_send()
        for f in range(NY):

            @pl.when(y != f)
            def _():
                sent(tg, ls.at[f])

    for m in range(3):
        wcopy(m).wait_send()
        gcopy(m).wait_send()
    for k in range(NY + 1):
        swap_rows(k).wait_send()

        @pl.when(column)
        def _():
            for d in range(1, 8):
                row_send(d, k).wait_send()

    for f in range(NY):
        swap_back(f).wait_send()
        for d in range(1, NX):
            back_send(d, f).wait_send()

        @pl.when(jnp.logical_not(column))
        def _():
            back_send(0, f).wait_send()

        @pl.when(column)
        def _():
            for slot in range(2):
                zback(mine(0, f), 1, slot, f).wait_send()

        @pl.when(source)
        def _():
            zback(mine(0, f), 1, 4, f).wait_send()

        @pl.when(relay)
        def _():
            for slot in range(2, 4):
                zback(mine(0, f), 1, slot, f).wait_send()

    for k in range(NY):
        for f in both(k):

            @pl.when(source)
            def _():
                for n in (1, -1):
                    zcopy(n, s_own, f).wait_send()

            @pl.when(relay)
            def _():
                for n in (1, -1, 2, -2, 3 if k < 2 else -3):
                    zcopy(n, s_own, f).wait_send()


def exchange(*operands):
    vmem = pl.BlockSpec(memory_space=pltpu.VMEM)
    whole = pl.BlockSpec(memory_space=pl.ANY)
    dma = pltpu.SemaphoreType.DMA
    return pl.pallas_call(
        kernel,
        out_shape=(
            jax.ShapeDtypeStruct((HID, D), BF16),
            jax.ShapeDtypeStruct((HID, D), BF16),
            jax.ShapeDtypeStruct((HID, D), BF16),
            jax.ShapeDtypeStruct((TOK, QD), BF16),
            jax.ShapeDtypeStruct((8, TOK), F32),
        ),
        in_specs=[vmem] * 4 + [whole] * 6 + [vmem] * 3,
        out_specs=(vmem,) * 5,
        scratch_shapes=[
            pltpu.VMEM((3, 2, HID, D), BF16),
            pltpu.VMEM((3, HH, D), BF16),
            pltpu.VMEM((3, HH, D), BF16),
            pltpu.VMEM((3, HID, D), BF16),
            pltpu.VMEM((NY, 4 * TOK, 2 * QD), BF16),
            pltpu.VMEM((4, 2 * EXPERTS, TOK), F32),
            pltpu.VMEM((8 * SRC, 2 * D + EXTRA), BF16),
            pltpu.VMEM((2 * ROWS, 2 * D + EXTRA), BF16),
            pltpu.VMEM((8 * SRC, 4 * TOK), BF16),
            pltpu.VMEM((4 * TOK, 8 * SRC), BF16),
            pltpu.VMEM((ROWS, HH), F32),
            pltpu.VMEM((ROWS, HH), F32),
            pltpu.VMEM((ROWS, HH), F32),
            pltpu.VMEM((4, ROWS, 1), F32),
            pltpu.VMEM((ROWS, HH), BF16),
            pltpu.VMEM((ROWS, HH), BF16),
            pltpu.VMEM((3, HH, 2 * ROWS), BF16),
            pltpu.VMEM((ROWS, D), F32),
            pltpu.VMEM((ROWS, D + EXTRA), BF16),
            pltpu.VMEM((ROWS, D + EXTRA), BF16),
            pltpu.VMEM((ROWS, D + EXTRA), BF16),
            pltpu.VMEM((8 * SRC, D + EXTRA), BF16),
            pltpu.VMEM((4 * TOK, D + EXTRA), BF16),
            pltpu.VMEM((5, TOK, D + EXTRA), BF16),
            pltpu.VMEM((2, TOK, D + EXTRA), BF16),
            pltpu.VMEM((TOK, D + EXTRA), BF16),
            pltpu.VMEM((TOK, 2 * QD), BF16),
            pltpu.VMEM((TOK, QD), BF16),
            pltpu.VMEM((TOK, EXTRA), BF16),
            dma((3, 2)),
            dma((3,)),
            dma((3,)),
            dma((3,)),
            dma((3,)),
            dma,
            dma((NY,)),
            dma((2, 3, 5)),
            dma((4, 5)),
            dma((NY + 1, 8)),
            dma((NY + 1, NX)),
            dma((NY + 1,)),
            dma((NY + 1,)),
            dma((NY,)),
            dma((NY,)),
            dma((NY, NX)),
            dma((NY, 8)),
            dma((NY, 5)),
            dma((NY, 5)),
            dma((2 * NY,)),
            dma((2,)),
        ],
        compiler_params=pltpu.CompilerParams(
            collective_id=0, has_side_effects=True, vmem_limit_bytes=64 * 1024 * 1024 - 256 * 1024
        ),
    )(*operands)


def body(
    tokens, cotangent, route_weights, routes,
    grid_gate, latent_gate, scale_gate,
    grid_up, latent_up, scale_up,
    grid_down, latent_down, scale_down,
):
    grad_gate, grad_up, grad_down, token_grad, route_grad = exchange(
        tokens, cotangent, routes.T, route_weights.T,
        grid_gate[0], latent_gate[0], grid_up[0], latent_up[0], grid_down[0], latent_down[0],
        scale_gate, scale_up, scale_down,
    )
    return (
        grad_gate.astype(F32)[None], grad_up.astype(F32)[None], grad_down.astype(F32)[None],
        token_grad, route_grad.T,
    )


def solution(mesh):
    return jax.shard_map(
        body,
        mesh=mesh,
        in_specs=(
            P("ep", "tp"), P("ep", "tp"), P("ep", None), P("ep", None),
            P("ep", "tp", None), P("ep", "tp", None), P("ep", "tp"),
            P("ep", "tp", None), P("ep", "tp", None), P("ep", "tp"),
            P("ep", "tp", None), P("ep", "tp", None), P("ep", None),
        ),
        out_specs=(
            P("ep", "tp", None), P("ep", "tp", None), P("ep", "tp", None), P("ep", "tp"), P("ep", None),
        ),
        check_vma=False,
    )
```

time: 511 us -> 154 us (0.30)
  waiting for transfers between devices: 254 us -> 0 us
  Pallas kernels: 0 us -> 147 us
  blocking collectives: 119 us -> 0 us
  local copies, waits for them, and re-layouts: 50 us -> 1.26 us
  matrix products: 33.1 us -> 0 us
  other arithmetic: 27.3 us -> 4.8 us
  between operations: 14.5 us -> 0.66 us
  starting transfers between devices: 10.7 us -> 0 us
    pallas_call x0 -> x1, Pallas kernels: none -> 147 us  [exchange(): pl.pallas_call(kernel, out_shape=(jax.ShapeDtypeStruct((HID, D), BF16), j...]
    all_to_all x3 -> x0, blocking collectives: 119 us -> none  [the longest x1 92.6 us: sent_together(): lax.all_to_all(both, axis, split_axis=split_dim, concat_axis=concat_dim,...]
    all_gather x1 -> x0, waiting for transfers between devices: 117 us -> none  [side_by_side(): lax.all_gather(both, axis, axis=dim, tiled=True)]
    reduce_scatter x1 -> x0, waiting for transfers between devices: 90 us -> none  [body(): share = lax.psum_scatter(back_rows, 'tp', scatter_dimension=2, tiled=True)]
    all_to_all x1 -> x0, waiting for transfers between devices: 47.4 us -> none  [body(): lax.all_to_all(share, 'ep', split_axis=0, concat_axis=0, tiled=True)]
    dot_general x8 -> x0, matrix products: 33.1 us -> none  [the longest x1 6.59 us: expert_backward(): jnp.dot(grad_upper, w_up, preferred_element_type=jnp.float32)]
    gather x5 -> x0, local copies, waits for them, and re-layouts: 30.1 us -> none  [the longest x1 9.46 us: body(): send_weights = weights_pad[table].reshape(experts, capacity)]
    another operation x3 -> x0, other arithmetic: 18.2 us -> none
  transfers between devices with their start and end apart: 3 -> 0, of which waited for: 3 -> 0; matrix products, arithmetic and copies ran while one was open for 6% -> 0% of each run, Pallas kernels for 0% -> 0%
where the time goes in v2:
time: 154 us; the launch traced here: 153 us
  Pallas kernels  147 us (95%)
  other arithmetic  4.8 us (3%)
    pallas_call x1, Pallas kernels, exchange(): pl.pallas_call(kernel, out_shape=(jax.ShapeDtypeStruct((HID, D), BF16), j...  147 us
    broadcast_in_dim x1, other arithmetic, body(): grad_down.astype(F32)[None]  3.48 us

profile of v2, /device:TPU:38, one launch (start us, length us, event | category | flops | bytes accessed | tf_op | source)
XLA Modules:
  0.0 153.4 jit_solution(17194403010683867995)
XLA Ops:
  0.6 146.7 %shard_map.164 = (bf16[192,2048]{1,0:T(8,128)(2,1)}, bf16[192,2048]{1,0:T(8,128)(2,1)}, bf16[192,2048]{1,0:T(8,128)(2,1)}, bf16[128,512]{1,0:T(8,128)(2,1)}, f32[8,128]{1,0:T(8,128)}) custom-call(bf16[128,512]{1,0:T(8,128)(2,1)} %tok_ref.1, bf16[128,512]{1,0:T(8,128)(2,1)} %cot_ref.1, s32[8,128]{1,0:T(8,128)} %bitcast.24, bf16[8,128]{1,0:T(8,128)(2,1)} %bitcast.26, ...), custom_call_target="tpu_custom_call" | custom-call | tf_op jit(solution)/shard_map/pallas_call | solution.py:568
  147.3 0.0 copy-start
  147.4 3.5 %bitcast_convert_fusion = (f32[1,192,2048]{2,1,0:T(8,128)}, f32[1,192,2048]{2,1,0:T(8,128)}) fusion(bf16[192,2048]{1,0:T(8,128)(2,1)} %get-tuple-element.12, bf16[192,2048]{1,0:T(8,128)(2,1)} %get-tuple-element.11), kind=kLoop, calls=%fused_computation | loop fusion | flops 786432 | bytes 4718592 | tf_op jit(solution)/shard_map/broadcast_in_dim | solution.py:649
  150.8 0.0 copy-start.1
  150.8 0.0 copy-start.2
  150.8 0.0 copy-done
  150.8 1.3 bitcast_convert_fusion.2
  152.2 0.0 copy-done.1
  152.2 0.7 copy.20
  152.8 0.0 copy-done.2
  152.8 0.6 copy.21
Async XLA Ops:
  147.3 3.5 %copy-start = (bf16[192,2048]{1,0:T(8,128)(2,1)S(1)}, bf16[192,2048]{1,0:T(8,128)(2,1)}, u32[]{:S(2)}) copy-start(bf16[192,2048]{1,0:T(8,128)(2,1)} %get-tuple-element.10) | copy-start | bytes 2359300
  150.8 1.3 copy-start.1
  150.8 2.0 %copy-start.2 = (f32[8,128]{1,0:T(8,128)S(1)}, f32[8,128]{1,0:T(8,128)}, u32[]{:S(2)}) copy-start(f32[8,128]{1,0:T(8,128)} %get-tuple-element.14) | copy-start | bytes 12292

commit v3 on v2

--- a/solution.py
+++ b/solution.py
@@ -29,6 +29,8 @@
 
 
 ORDER = (0, 1, 3, 2)
+PIECES = 2 * NY
+AHEAD = 2
 
 
 def going(f, h):
@@ -36,8 +38,8 @@
     return slice(at, at + QD)
 
 
-def lanes_of(f):
-    return pl.ds(pl.multiple_of(EXTRA + 2 * QD * f, 128), 2 * QD)
+def lanes_of(f, h):
+    return pl.ds(pl.multiple_of(EXTRA + 2 * QD * f + QD * h, 128), QD)
 
 
 def coming(f):
@@ -52,7 +54,7 @@
     tok_ref, cot_ref, rt_ref, wt_ref, gg_ref, lg_ref, gu_ref, lu_ref, gd_ref, ld_ref, sg_ref, su_ref, sd_ref,
     og_ref, ou_ref, od_ref, tgrad_ref, rgrad_ref,
     raw, wf, grad, rr, blk, aux, sendbuf, rows, smat, smt, gs, us, bh, sco, dg, du, lt,
-    bown, bsend, bgot, br, rb, part, zb, zt, fb, stage, tg, sc,
+    bown, bsend, bgot, br, rb, part, zb, zt, fb, tg, sc,
     rawsem, ws, wr, gsend, grecv, ys, yr, zs, zr, xs, xr, fs, fr, es, er, bs, brr, zbs, zbr, ls, lr,
 ):
     i, y = lax.axis_index("ep"), lax.axis_index("tp")
@@ -83,10 +85,10 @@
         )
 
     def arrived(dst, recv):
-        remote(dst, dst, ys, recv, (i, up(1))).wait_recv()
+        remote(dst, dst, ys.at[0], recv, (i, up(1))).wait_recv()
 
     def sent(src, send):
-        remote(src, src, send, yr.at[0], (i, up(1))).wait_send()
+        remote(src, src, send, yr.at[0, 0], (i, up(1))).wait_send()
 
     raws = ((gg_ref, lg_ref), (gu_ref, lu_ref), (gd_ref, ld_ref))
     for m in range(3):
@@ -101,8 +103,6 @@
     for d in range(1, 8):
         pl.semaphore_signal(barrier, inc=1, device_id=(8 * z + lax.rem(own + d, 8), y), device_id_type=MESH)
 
-    stage[:, 0:QD] = tok_ref[...]
-    stage[:, QD:] = cot_ref[...]
     s_own = z // 2
     order = [up(d) for d in ORDER]
 
@@ -126,32 +126,50 @@
 
     pl.semaphore_wait(barrier, 3 + 6 + 7)
 
-    @pl.when(jnp.logical_not(owner))
-    def _():
-        remote(stage, block(s_own, y), ys, yr.at[y], (i, yb)).start()
-
-    def piece(s, f):
-        return aux.at[s] if f is None else block(s, f)
-
-    def zcopy(n, s, f):
-        at = 4 if f is None else f
-        return remote(piece(s, f), piece(s, f), zs.at[int(n < 0), abs(n) - 1, at], zr.at[s, at], zdev(n))
-
-    def zgot(s, f):
-        arrived(piece(s, f), zr.at[s, 4 if f is None else f])
-
-    def give(f):
-        zcopy(1, s_own, f).start()
-        zcopy(-1, s_own, f).start()
-
-    def both(k):
-        return (None, order[0]) if k == 0 else (order[k],)
+    halves = ((tok_ref, slice(0, QD)), (cot_ref, slice(QD, 2 * QD)))
+
+    def token_send(h):
+        src, lanes = halves[h]
+        return remote(src, block(s_own, y).at[:, lanes], ys.at[h], yr.at[y, h], (i, yb))
+
+    def token_keep(h):
+        src, lanes = halves[h]
+        return pltpu.make_async_copy(src, block(s_own, y).at[:, lanes], yr.at[y, h])
+
+    for h in range(2):
+
+        @pl.when(jnp.logical_not(owner))
+        def _():
+            token_send(h).start()
+
+        @pl.when(owner)
+        def _():
+            token_keep(h).start()
+
+    def piece(s, k):
+        if k == PIECES:
+            return aux.at[s]
+        return block(s, order[k // 2]).at[:, halves[k % 2][1]]
+
+    def zcopy(n, s, k):
+        return remote(piece(s, k), piece(s, k), zs.at[int(n < 0), abs(n) - 1, k], zr.at[s, k], zdev(n))
+
+    def zgot(s, k):
+        arrived(piece(s, k), zr.at[s, k])
+
+    def give(k):
+        zcopy(1, s_own, k).start()
+        zcopy(-1, s_own, k).start()
+
+    def with_extra(k):
+        return (PIECES, 0) if k == 0 else (k,)
 
     @pl.when(source)
     def _():
-        block(s_own, y)[...] = stage[...]
-        give(None)
-        give(y)
+        give(PIECES)
+        for h in range(2):
+            token_keep(h).wait()
+            give(h)
 
     diagonal = lax.broadcasted_iota(jnp.int32, (HID, HID), 0) == lax.broadcasted_iota(jnp.int32, (HID, HID), 1)
 
@@ -185,35 +203,33 @@
     soften(1)
     soften(2)
 
+    def give_next(k):
+        arrived(piece(s_own, k), yr.at[order[k // 2], k % 2])
+        give(k)
+
     @pl.when(source)
     def _():
-        for f in order[1:]:
-            arrived(block(s_own, f), yr.at[f])
-            give(f)
+        for k in range(2, AHEAD + 2):
+            give_next(k)
 
     def relay_piece(k):
-        for f in both(k):
-            zgot(zat(-1) // 2, f)
-            zcopy(1, zat(-1) // 2, f).start()
-            zcopy(2, zat(-1) // 2, f).start()
-            if k < 2:
-                zcopy(3, zat(-1) // 2, f).start()
-            zgot(zat(1) // 2, f)
-            zcopy(-1, zat(1) // 2, f).start()
-            zcopy(-2, zat(1) // 2, f).start()
-            if k >= 2:
-                zcopy(-3, zat(1) // 2, f).start()
+        for n, side in ((-1, 1), (1, -1)):
+            zgot(zat(n) // 2, k)
+            zcopy(side, zat(n) // 2, k).start()
+            zcopy(2 * side, zat(n) // 2, k).start()
+            if (side == 1) == (k % 2 == 0):
+                zcopy(3 * side, zat(n) // 2, k).start()
 
     @pl.when(relay)
     def _():
-        relay_piece(0)
-        relay_piece(1)
+        for k in (PIECES, *range(AHEAD)):
+            relay_piece(k)
 
     def rowpart(xsrc, lanes):
         return rows.at[pl.ds(pl.multiple_of(SRC * xsrc, SRC), SRC), lanes]
 
     def out_lanes(k):
-        return slice(0, EXTRA) if k == NY else lanes_of(order[k])
+        return slice(0, EXTRA) if k == PIECES else lanes_of(order[k // 2], k % 2)
 
     def row_send(d, k):
         j = lax.rem(own + d, 8)
@@ -227,28 +243,25 @@
             rows.at[0:ROWS, out_lanes(k)], rows.at[ROWS : 2 * ROWS, out_lanes(k)], fs.at[k], fr.at[k], (i, rpair)
         )
 
-    def with_extra(k):
-        return (NY, 0) if k == 0 else (k,)
-
     def forward(k):
         for g in with_extra(k):
             for xsrc in range(NX):
                 arrived(rowpart(xsrc, out_lanes(g)), xr.at[g, xsrc])
             swap_rows(g).start()
 
-    for k in range(NY):
+    for k in range(PIECES):
 
         @pl.when(source)
         def _():
-            for f in both(k):
+            for g in with_extra(k):
                 for n in (2, -2, 4):
-                    zgot(zat(n) // 2, f)
+                    zgot(zat(n) // 2, g)
 
         @pl.when(relay)
         def _():
-            for f in both(k):
+            for g in with_extra(k):
                 for n in (3, -3):
-                    zgot(zat(n) // 2, f)
+                    zgot(zat(n) // 2, g)
 
         @pl.when(column)
         def _():
@@ -262,22 +275,25 @@
                     smat[SRC * j : SRC * (j + 1), :] = jnp.where(chosen, 1.0, 0.0).astype(BF16)
                     gain = jnp.sum(jnp.where(chosen, gains[j : j + 1, :], 0.0), axis=1, keepdims=True)
                     sendbuf[SRC * j : SRC * (j + 1), 0:EXTRA] = jnp.broadcast_to(gain, (SRC, EXTRA)).astype(BF16)
-            f = order[k]
-            for h in range(2):
-                picked = dot_nn(smat[...], blk[f, :, QD * h : QD * (h + 1)])
-                sendbuf[:, pl.ds(pl.multiple_of(EXTRA + 2 * QD * f + QD * h, 128), QD)] = picked.astype(BF16)
+            picked = dot_nn(smat[...], blk[order[k // 2], :, halves[k % 2][1]])
+            sendbuf[:, out_lanes(k)] = picked.astype(BF16)
             for g in with_extra(k):
                 for d in range(8):
                     row_send(d, g).start()
 
+        @pl.when(source)
+        def _():
+            if k + AHEAD + 2 < PIECES:
+                give_next(k + AHEAD + 2)
+
         @pl.when(relay)
         def _():
-            if k + 2 < NY:
-                relay_piece(k + 2)
+            if k + AHEAD < PIECES:
+                relay_piece(k + AHEAD)
 
         if k >= 1:
             forward(k - 1)
-    forward(NY - 1)
+    forward(PIECES - 1)
 
     @pl.when(column)
     def _():
@@ -334,8 +350,8 @@
     hidden(0)
     for f in range(NY):
         bown[:, feature(f)] = back_of(f)
-    for k in range(NY + 1):
-        lanes = slice(0, EXTRA) if k == NY else lanes_of(lax.rem(rpair + ORDER[k], NY))
+    for k in range(PIECES + 1):
+        lanes = slice(0, EXTRA) if k == PIECES else lanes_of(lax.rem(rpair + ORDER[k // 2], NY), k % 2)
         arrived(rows.at[ROWS : 2 * ROWS, lanes], fr.at[k])
     hidden(1)
     for f in range(NY):
@@ -501,7 +517,8 @@
 
     @pl.when(jnp.logical_not(owner))
     def _():
-        sent(stage, ys)
+        for h in range(2):
+            token_send(h).wait_send()
 
     @pl.when(owner)
     def _():
@@ -516,7 +533,7 @@
     for m in range(3):
         wcopy(m).wait_send()
         gcopy(m).wait_send()
-    for k in range(NY + 1):
+    for k in range(PIECES + 1):
         swap_rows(k).wait_send()
 
         @pl.when(column)
@@ -547,18 +564,17 @@
             for slot in range(2, 4):
                 zback(mine(0, f), 1, slot, f).wait_send()
 
-    for k in range(NY):
-        for f in both(k):
-
-            @pl.when(source)
-            def _():
-                for n in (1, -1):
-                    zcopy(n, s_own, f).wait_send()
-
-            @pl.when(relay)
-            def _():
-                for n in (1, -1, 2, -2, 3 if k < 2 else -3):
-                    zcopy(n, s_own, f).wait_send()
+    for k in range(PIECES + 1):
+
+        @pl.when(source)
+        def _():
+            for n in (1, -1):
+                zcopy(n, s_own, k).wait_send()
+
+        @pl.when(relay)
+        def _():
+            for n in (1, -1, 2, -2, 3 if k % 2 == 0 else -3):
+                zcopy(n, s_own, k).wait_send()
 
 
 def exchange(*operands):
@@ -574,7 +590,7 @@
             jax.ShapeDtypeStruct((TOK, QD), BF16),
             jax.ShapeDtypeStruct((8, TOK), F32),
         ),
-        in_specs=[vmem] * 4 + [whole] * 6 + [vmem] * 3,
+        in_specs=[whole] * 2 + [vmem] * 2 + [whole] * 6 + [vmem] * 3,
         out_specs=(vmem,) * 5,
         scratch_shapes=[
             pltpu.VMEM((3, 2, HID, D), BF16),
@@ -603,7 +619,6 @@
             pltpu.VMEM((5, TOK, D + EXTRA), BF16),
             pltpu.VMEM((2, TOK, D + EXTRA), BF16),
             pltpu.VMEM((TOK, D + EXTRA), BF16),
-            pltpu.VMEM((TOK, 2 * QD), BF16),
             pltpu.VMEM((TOK, QD), BF16),
             pltpu.VMEM((TOK, EXTRA), BF16),
             dma((3, 2)),
@@ -611,14 +626,14 @@
             dma((3,)),
             dma((3,)),
             dma((3,)),
-            dma,
-            dma((NY,)),
-            dma((2, 3, 5)),
-            dma((4, 5)),
-            dma((NY + 1, 8)),
-            dma((NY + 1, NX)),
-            dma((NY + 1,)),
-            dma((NY + 1,)),
+            dma((2,)),
+            dma((NY, 2)),
+            dma((2, 3, PIECES + 1)),
+            dma((4, PIECES + 1)),
+            dma((PIECES + 1, 8)),
+            dma((PIECES + 1, NX)),
+            dma((PIECES + 1,)),
+            dma((PIECES + 1,)),
             dma((NY,)),
             dma((NY,)),
             dma((NY, NX)),

time: 154 us -> 147 us (0.955)
  the two profiles are of different devices: /device:TPU:38 before, /device:TPU:16 now
where the time goes in v3:
time: 147 us
  Pallas kernels  140 us (95%)
  other arithmetic  4.8 us (3%)
    pallas_call x1, Pallas kernels, exchange(): pl.pallas_call(kernel, out_shape=(jax.ShapeDtypeStruct((HID, D), BF16), j...  140 us
    broadcast_in_dim x1, other arithmetic, body(): grad_down.astype(F32)[None]  3.48 us

profile of v3, /device:TPU:16, one launch (start us, length us, event | category | flops | bytes accessed | tf_op | source)
XLA Modules:
  0.0 146.5 jit_solution(2178944314088064859)
XLA Ops:
  0.6 139.8 %shard_map.164 = (bf16[192,2048]{1,0:T(8,128)(2,1)}, bf16[192,2048]{1,0:T(8,128)(2,1)}, bf16[192,2048]{1,0:T(8,128)(2,1)}, bf16[128,512]{1,0:T(8,128)(2,1)}, f32[8,128]{1,0:T(8,128)}) custom-call(bf16[128,512]{1,0:T(8,128)(2,1)} %tok_ref.1, bf16[128,512]{1,0:T(8,128)(2,1)} %cot_ref.1, s32[8,128]{1,0:T(8,128)} %bitcast.24, bf16[8,128]{1,0:T(8,128)(2,1)} %bitcast.26, ...), custom_call_target="tpu_custom_call" | custom-call | tf_op jit(solution)/shard_map/pallas_call | solution.py:584
  140.5 0.0 copy-start
  140.5 3.5 %bitcast_convert_fusion = (f32[1,192,2048]{2,1,0:T(8,128)}, f32[1,192,2048]{2,1,0:T(8,128)}) fusion(bf16[192,2048]{1,0:T(8,128)(2,1)} %get-tuple-element.12, bf16[192,2048]{1,0:T(8,128)(2,1)} %get-tuple-element.11), kind=kLoop, calls=%fused_computation | loop fusion | flops 786432 | bytes 4718592 | tf_op jit(solution)/shard_map/broadcast_in_dim | solution.py:664
  144.0 0.0 copy-start.1
  144.0 0.0 copy-start.2
  144.0 0.0 copy-done
  144.0 1.3 bitcast_convert_fusion.2
  145.3 0.0 copy-done.1
  145.3 0.7 copy.20
  145.9 0.0 copy-done.2
  145.9 0.6 copy.21
Async XLA Ops:
  140.5 3.5 %copy-start = (bf16[192,2048]{1,0:T(8,128)(2,1)S(1)}, bf16[192,2048]{1,0:T(8,128)(2,1)}, u32[]{:S(2)}) copy-start(bf16[192,2048]{1,0:T(8,128)(2,1)} %get-tuple-element.10) | copy-start | bytes 2359300
  144.0 1.3 copy-start.1
  144.0 2.0 %copy-start.2 = (f32[8,128]{1,0:T(8,128)S(1)}, f32[8,128]{1,0:T(8,128)}, u32[]{:S(2)}) copy-start(f32[8,128]{1,0:T(8,128)} %get-tuple-element.14) | copy-start | bytes 12292

commit v4 on v3

--- a/solution.py
+++ b/solution.py
@@ -313,6 +313,7 @@
                 total = term if total is None else total + term
             out[...] = total
 
+    def gradients(r):
         @pl.loop(0, ROWS // 128)
         def _(t):
             at = pl.multiple_of(128 * t, 128)
@@ -348,12 +349,18 @@
         return remote(bsend.at[:, coming(f)], bgot.at[:, coming(f)], es.at[f], er.at[f], (i, rpair))
 
     hidden(0)
+    gradients(0)
     for f in range(NY):
         bown[:, feature(f)] = back_of(f)
-    for k in range(PIECES + 1):
-        lanes = slice(0, EXTRA) if k == PIECES else lanes_of(lax.rem(rpair + ORDER[k // 2], NY), k % 2)
-        arrived(rows.at[ROWS : 2 * ROWS, lanes], fr.at[k])
-    hidden(1)
+    arrived(rows.at[ROWS : 2 * ROWS, 0:EXTRA], fr.at[PIECES])
+    for k in range(PIECES):
+        f = lax.rem(rpair + ORDER[k // 2], NY)
+        arrived(rows.at[ROWS : 2 * ROWS, lanes_of(f, k % 2)], fr.at[k])
+        here = rows[ROWS : 2 * ROWS, lanes_of(f, k % 2)]
+        for out, m in ((bh, 2),) if k % 2 else ((gs, 0), (us, 1)):
+            term = dot_nt(here, wf[m, :, pl.ds(pl.multiple_of(QD * f, QD), QD)])
+            out[...] = term if k < 2 else out[...] + term
+    gradients(1)
     for f in range(NY):
         bsend[:, feature(f)] = back_of(f).astype(BF16)
         if f == NY - 1:

time: 147 us -> 144 us (0.980)
  the two profiles are of different devices: /device:TPU:16 before, /device:TPU:22 now
where the time goes in v4:
time: 144 us
  Pallas kernels  138 us (96%)
  other arithmetic  4.8 us (3%)
    pallas_call x1, Pallas kernels, exchange(): pl.pallas_call(kernel, out_shape=(jax.ShapeDtypeStruct((HID, D), BF16), j...  138 us
    broadcast_in_dim x1, other arithmetic, body(): grad_down.astype(F32)[None]  3.48 us

profile of v4, /device:TPU:22, one launch (start us, length us, event | category | flops | bytes accessed | tf_op | source)
XLA Modules:
  0.0 144.3 jit_solution(5296636396447704515)
XLA Ops:
  0.6 137.6 %shard_map.164 = (bf16[192,2048]{1,0:T(8,128)(2,1)}, bf16[192,2048]{1,0:T(8,128)(2,1)}, bf16[192,2048]{1,0:T(8,128)(2,1)}, bf16[128,512]{1,0:T(8,128)(2,1)}, f32[8,128]{1,0:T(8,128)}) custom-call(bf16[128,512]{1,0:T(8,128)(2,1)} %tok_ref.1, bf16[128,512]{1,0:T(8,128)(2,1)} %cot_ref.1, s32[8,128]{1,0:T(8,128)} %bitcast.24, bf16[8,128]{1,0:T(8,128)(2,1)} %bitcast.26, ...), custom_call_target="tpu_custom_call" | custom-call | tf_op jit(solution)/shard_map/pallas_call | solution.py:591
  138.2 0.0 copy-start
  138.2 3.5 %bitcast_convert_fusion = (f32[1,192,2048]{2,1,0:T(8,128)}, f32[1,192,2048]{2,1,0:T(8,128)}) fusion(bf16[192,2048]{1,0:T(8,128)(2,1)} %get-tuple-element.12, bf16[192,2048]{1,0:T(8,128)(2,1)} %get-tuple-element.11), kind=kLoop, calls=%fused_computation | loop fusion | flops 786432 | bytes 4718592 | tf_op jit(solution)/shard_map/broadcast_in_dim | solution.py:671
  141.7 0.0 copy-start.1
  141.7 0.0 copy-start.2
  141.7 0.0 copy-done
  141.7 1.3 bitcast_convert_fusion.2
  143.0 0.0 copy-done.1
  143.0 0.7 copy.20
  143.7 0.0 copy-done.2
  143.7 0.6 copy.21
Async XLA Ops:
  138.2 3.5 %copy-start = (bf16[192,2048]{1,0:T(8,128)(2,1)S(1)}, bf16[192,2048]{1,0:T(8,128)(2,1)}, u32[]{:S(2)}) copy-start(bf16[192,2048]{1,0:T(8,128)(2,1)} %get-tuple-element.10) | copy-start | bytes 2359300
  141.7 1.3 copy-start.1
  141.7 2.0 %copy-start.2 = (f32[8,128]{1,0:T(8,128)S(1)}, f32[8,128]{1,0:T(8,128)}, u32[]{:S(2)}) copy-start(f32[8,128]{1,0:T(8,128)} %get-tuple-element.14) | copy-start | bytes 12292
